TPU v7x, 256 devices: a whole 4x4x8 slice. The times are simulated.
256 devices in a mesh: dp: 16 (over y, x), expert: 16 (over z, core).
Axes of the slice: x: 4, y: 4, z: 8, core: 2. Of those that a mesh axis runs over, the one named last changes fastest.
Arguments:
- tokens: bfloat16 [32768, 2048], P(('dp', 'expert')), may hold values from -6 to 6
- initial_expert_index: int32 [32768, 4], P(('dp', 'expert')), may hold values from 0 to 31, all different within a row; in each aligned block of 128 rows (0 to 127, 128 to 255, ...) at most 18 rows name the same one
- pruned_expert_index: int32 [32768, 4], P(('dp', 'expert')), may hold values from 0 to 15, all different within a row; in each aligned block of 128 rows (0 to 127, 128 to 255, ...) at most 36 rows name the same one
- initial_router_scores: float32 [32768, 4], P(('dp', 'expert')), may hold values from 0.05 to 1
- pruned_router_scores: float32 [32768, 4], P(('dp', 'expert')), may hold values from 0.05 to 1
- gate_weight: bfloat16 [32, 2048, 768], P('expert', 'dp'), may hold values from -0.125 to 0.125
- up_weight: bfloat16 [32, 2048, 768], P('expert', 'dp'), may hold values from -0.125 to 0.125
- down_weight: bfloat16 [32, 768, 2048], P('expert', None, 'dp'), may hold values from -0.21875 to 0.21875
- adapter_first_weight: float32 [16, 768, 64], P('expert'), may hold values from -0.21875 to 0.21875
- adapter_second_weight: float32 [16, 64, 2048], P('expert'), may hold values from -0.75 to 0.75
Outputs:
- grad_a: float32 [16, 768, 64], P('expert', 'dp')
- grad_b: float32 [16, 64, 2048], P('expert', None, 'dp')
Inputs may be any that keep to these rules, and one draw needn't show every extreme that they name: `initial_expert_index`: the 4 entries of a row differ. In each aligned block of 128 rows no expert is named more than 18 times, a bound that some block reaches. `pruned_expert_index`: the 4 entries of a row differ. In each aligned block of 128 rows no expert is named more than 36 times, a bound that some block reaches.
All inputs are finite; a program needn't handle non-finite values.
Results may differ from a plain program's by a relative error of at most 0.0029.
Values may be sent and summed in bfloat16 or wider, within the bound.
A program may use at most 128 MiB of HBM per device.

v0:
```python
import jax
import jax.numpy as jnp
from jax import lax
from jax.sharding import PartitionSpec as P


def route_tables(route_ids, weight, num_experts, capacity):
    tok_rows, top_count = route_ids.shape
    shares = weight / jnp.sum(weight, axis=1, keepdims=True)
    flat_ids = route_ids.reshape(-1)
    hit_table = (flat_ids[:, None] == jnp.arange(num_experts, dtype=jnp.int32)[None, :]).astype(
        jnp.int32
    )
    slot_index = jnp.sum(hit_table * (jnp.cumsum(hit_table, axis=0) - 1), axis=1)
    dest_index = flat_ids * capacity + slot_index
    owner_token = jnp.arange(tok_rows * top_count, dtype=jnp.int32) // top_count
    slot_token = jnp.zeros(num_experts * capacity, jnp.int32).at[dest_index].set(owner_token)
    slot_weight = (
        jnp.zeros(num_experts * capacity, jnp.float32).at[dest_index].set(shares.reshape(-1))
    )
    return (dest_index, shares, slot_token, slot_weight)


def combine_rows(back_rows, dest_index, shares, width):
    picked = jnp.take(back_rows.reshape(-1, width), dest_index, axis=0)
    picked = picked.reshape(shares.shape[0], shares.shape[1], width).astype(jnp.float32)
    return jnp.sum(picked * shares[:, :, None], axis=1)


def shards(
    tokens,
    initial_expert_index,
    pruned_expert_index,
    initial_router_scores,
    pruned_router_scores,
    gate_weight,
    up_weight,
    down_weight,
    adapter_first_weight,
    adapter_second_weight,
):
    peers = lax.axis_size("expert")
    tok_rows, width = tokens.shape
    top_count = initial_expert_index.shape[1]
    local_experts = gate_weight.shape[0]
    resident_pruned_experts = adapter_first_weight.shape[0]
    all_experts = local_experts * peers
    all_pruned = resident_pruned_experts * peers
    cap_frozen = 9 * tok_rows * top_count // (8 * all_experts)
    cap_pruned = 9 * tok_rows * top_count // (8 * all_pruned)
    frozen_dest, frozen_share, frozen_tok, frozen_wts = route_tables(
        initial_expert_index, initial_router_scores, all_experts, cap_frozen
    )
    pruned_dest, pruned_share, pruned_token_rows, pruned_gate_weights = route_tables(
        pruned_expert_index, pruned_router_scores, all_pruned, cap_pruned
    )
    frozen_send = jnp.take(tokens, frozen_tok, axis=0).reshape(
        peers, local_experts * cap_frozen, width
    )
    pruned_send = jnp.take(tokens, pruned_token_rows, axis=0).reshape(
        peers, resident_pruned_experts * cap_pruned, width
    )
    frozen_recv = lax.all_to_all(frozen_send, "expert", split_axis=0, concat_axis=0, tiled=True)
    pruned_recv = lax.all_to_all(pruned_send, "expert", split_axis=0, concat_axis=0, tiled=True)
    gate_full, up_full, down_full = (
        lax.all_gather(gate_weight, "dp", axis=1, tiled=True),
        lax.all_gather(up_weight, "dp", axis=1, tiled=True),
        lax.all_gather(down_weight, "dp", axis=2, tiled=True),
    )
    frozen_in = frozen_recv.reshape(peers, local_experts, cap_frozen, width)
    gate_part = jnp.einsum(
        "secd,edf->secf", frozen_in, gate_full, preferred_element_type=jnp.float32
    )
    up_part = jnp.einsum("secd,edf->secf", frozen_in, up_full, preferred_element_type=jnp.float32)
    frozen_hidden = (jax.nn.silu(gate_part) * up_part).astype(jnp.bfloat16)
    frozen_out = jnp.einsum(
        "secf,efd->secd", frozen_hidden, down_full, preferred_element_type=jnp.float32
    ).astype(jnp.bfloat16)
    pruned_in = pruned_recv.reshape(peers, resident_pruned_experts, cap_pruned, width)
    gate_keep = gate_full[0::2]
    up_keep = up_full[0::2]
    down_keep = down_full[0::2]
    gate_part = jnp.einsum(
        "spcd,pdf->spcf", pruned_in, gate_keep, preferred_element_type=jnp.float32
    )
    up_part = jnp.einsum("spcd,pdf->spcf", pruned_in, up_keep, preferred_element_type=jnp.float32)
    pruned_hidden = (jax.nn.silu(gate_part) * up_part).astype(jnp.bfloat16)
    hidden_full_width = lax.optimization_barrier(pruned_hidden).astype(jnp.float32)
    lowrank_hidden = jnp.einsum(
        "wqmh,qhi->wqmi", hidden_full_width, adapter_first_weight, precision=lax.Precision.HIGHEST
    )
    base = jnp.einsum(
        "spcf,pfd->spcd", pruned_hidden, down_keep, preferred_element_type=jnp.float32
    )
    output_error = jnp.einsum(
        "ywqo,won->ywqn", lowrank_hidden, adapter_second_weight, precision=lax.Precision.HIGHEST
    )
    pruned_out = (base + output_error).astype(jnp.bfloat16)
    frozen_back, pruned_back = (
        lax.all_to_all(
            frozen_out.reshape(peers, local_experts * cap_frozen, width),
            "expert",
            split_axis=0,
            concat_axis=0,
            tiled=True,
        ),
        lax.all_to_all(
            pruned_out.reshape(peers, resident_pruned_experts * cap_pruned, width),
            "expert",
            split_axis=0,
            concat_axis=0,
            tiled=True,
        ),
    )
    target = combine_rows(frozen_back, frozen_dest, frozen_share, width)
    pruned_estimate = combine_rows(pruned_back, pruned_dest, pruned_share, width)
    residual = pruned_estimate - target
    grad_send = (
        jnp.take(residual, pruned_token_rows, axis=0) * pruned_gate_weights[:, None]
    ).astype(jnp.bfloat16)
    grad_recv = lax.all_to_all(
        grad_send.reshape(peers, resident_pruned_experts * cap_pruned, width),
        "expert",
        split_axis=0,
        concat_axis=0,
        tiled=True,
    )
    gradient_hidden_full = grad_recv.reshape(
        peers, resident_pruned_experts, cap_pruned, width
    ).astype(jnp.float32)
    part_b = jnp.einsum(
        "spcr,spcd->prd", lowrank_hidden, gradient_hidden_full, precision=lax.Precision.HIGHEST
    )
    backward_lowrank = jnp.einsum(
        "qgub,gkb->qguk",
        gradient_hidden_full,
        adapter_second_weight,
        precision=lax.Precision.HIGHEST,
    )
    part_a = jnp.einsum(
        "spcf,spcr->pfr", hidden_full_width, backward_lowrank, precision=lax.Precision.HIGHEST
    )
    sum_a, sum_b = lax.psum((part_a, part_b), "dp")
    groups = lax.axis_size("dp")
    position = lax.axis_index("dp")
    share_ff = part_a.shape[1] // groups
    share_width = part_b.shape[2] // groups
    grad_a = lax.dynamic_slice_in_dim(sum_a, position * share_ff, share_ff, 1)
    grad_b = lax.dynamic_slice_in_dim(sum_b, position * share_width, share_width, 2)
    return (grad_a, grad_b)


def solution(mesh):
    placed = (
        P(("dp", "expert"), None),
        P(("dp", "expert"), None),
        P(("dp", "expert"), None),
        P(("dp", "expert"), None),
        P(("dp", "expert"), None),
        P("expert", "dp", None),
        P("expert", "dp", None),
        P("expert", None, "dp"),
        P("expert", None, None),
        P("expert", None, None),
    )
    return jax.shard_map(
        shards,
        mesh=mesh,
        in_specs=placed,
        out_specs=(P("expert", "dp", None), P("expert", None, "dp")),
        check_vma=False,
    )
```

profile of v0, /device:TPU:1, one launch (start us, length us, event | category | flops | bytes accessed | tf_op | source)
XLA Modules:
  0.0 585.8 jit_solution(12018079329480182576)
XLA Ops:
  15.4 4.0 gather_fusion.3
  23.5 10.1 %all-to-all-start.2 = ((bf16[16,36,2048]{2,1,0:T(8,128)(2,1)}), bf16[16,36,2048]{2,1,0:T(8,128)(2,1)S(1)}, u32[]{:S(2)}, u32[]{:S(2)}) async-start(bf16[16,36,2048]{2,1,0:T(8,128)(2,1)} %reshape.217), calls=%async_computation.2 | async-start | bytes 5242880 | tf_op jit(solution)/shard_map/all_to_all | solution.py:63
  38.1 4.0 gather_fusion.1
  42.2 3.4 broadcast_select_fusion.1
  45.6 4.1 reshape.207
  49.7 43.5 %all-to-all-done.2 = bf16[16,36,2048]{2,1,0:T(8,128)(2,1)S(1)} async-done(((bf16[16,36,2048]{2,1,0:T(8,128)(2,1)}), bf16[16,36,2048]{2,1,0:T(8,128)(2,1)S(1)}, u32[]{:S(2)}, u32[]{:S(2)}) %all-to-all-start.2) | async-done | bytes 2359328 | tf_op jit(solution)/shard_map/all_to_all | solution.py:63
  93.2 6.2 %all-to-all-start = ((bf16[16,36,2048]{2,1,0:T(8,128)(2,1)}), bf16[16,36,2048]{2,1,0:T(8,128)(2,1)}, u32[]{:S(2)}, u32[]{:S(2)}) async-start(bf16[16,36,2048]{2,1,0:T(8,128)(2,1)} %reshape.207), calls=%async_computation | async-start | bytes 5242880 | tf_op jit(solution)/shard_map/all_to_all | solution.py:64
  102.1 8.4 %fusion.4 = f32[2,16,18,768]{3,2,1,0:T(8,128)} fusion(bf16[2,2048,768]{2,1,0:T(8,128)(2,1)} %all-gather.4.cloned.1.call-done, bf16[16,2,18,2048]{3,0,2,1:T(8,128)(2,1)} %bitcast.153), kind=kOutput, calls=%fused_computation.12 | convolution fusion | flops 1811939328 | bytes 10420224 | tf_op jit(solution)/shard_map/secd,edf->secf/dot_general | solution.py:71
  110.4 42.9 %all-gather.8.cloned.1.call-done = bf16[2,768,2048]{2,1,0:T(8,128)(2,1)} async-done(((bf16[2,768,128]{2,1,0:T(8,128)(2,1)}), bf16[2,768,2048]{2,1,0:T(8,128)(2,1)}) %all-gather.8.cloned.1.call-update) | async-done | bytes 6291472 | tf_op jit(solution)/shard_map/all_gather | solution.py:68
  153.3 69.4 %all-gather.6.cloned.1.call-done = bf16[2,2048,768]{2,1,0:T(8,128)(2,1)} async-done(((bf16[2,128,768]{2,1,0:T(8,128)(2,1)}), bf16[2,2048,768]{2,1,0:T(8,128)(2,1)}) %all-gather.6.cloned.1.call-update) | async-done | bytes 6291472 | tf_op jit(solution)/shard_map/all_gather | solution.py:67
  222.7 12.9 %fusion.14 = bf16[16,2,18,2048]{3,2,0,1:T(8,128)(2,1)} fusion(bf16[2,768,2048]{2,1,0:T(8,128)(2,1)} %all-gather.8.cloned.1.call-done, f32[2,16,18,768]{3,2,1,0:T(8,128)} %fusion.4, bf16[2,2048,768]{2,1,0:T(8,128)(2,1)} %all-gather.6.cloned.1.call-done, bf16[16,2,18,2048]{3,0,2,1:T(8,128)(2,1)S(1)} %bitcast.154), kind=kOutput, calls=%fused_computation.27 | convolution fusion | flops 3627712512 | bytes 19070976 | tf_op jit(solution)/shard_map/secf,efd->secd/dot_general | solution.py:76
  235.6 3.2 copy.43
  238.8 2.8 copy.44
  241.6 7.9 %all-to-all-start.3 = ((bf16[16,36,2048]{2,1,0:T(8,128)(2,1)}), bf16[16,36,2048]{2,1,0:T(8,128)(2,1)S(1)}, u32[]{:S(2)}, u32[]{:S(2)}) async-start(bf16[16,36,2048]{2,1,0:T(8,128)(2,1)} %copy.44), calls=%async_computation.3 | async-start | bytes 5242880 | tf_op jit(solution)/shard_map/all_to_all | solution.py:100
  249.4 5.0 fusion.13
  254.5 5.2 fusion.21
  262.9 5.9 %add_convert_fusion = bf16[16,36,2048]{2,1,0:T(8,128)(2,1)} fusion(f32[16,36,2048]{2,1,0:T(8,128)S(1)} %fusion.11, f32[16,36,64]{2,1,0:T(8,128)S(1)} %fusion.36, f32[1,64,2048]{2,1,0:T(8,128)S(1)} %copy-done.6), kind=kOutput, calls=%fused_computation.15 | convolution fusion | flops 908328960 | bytes 7749632 | tf_op jit(solution)/shard_map/ywqo,won->ywqn/dot_general | solution.py:95
  268.8 40.2 %all-to-all-done.3 = bf16[16,36,2048]{2,1,0:T(8,128)(2,1)S(1)} async-done(((bf16[16,36,2048]{2,1,0:T(8,128)(2,1)}), bf16[16,36,2048]{2,1,0:T(8,128)(2,1)S(1)}, u32[]{:S(2)}, u32[]{:S(2)}) %all-to-all-start.3) | async-done | bytes 2359328 | tf_op jit(solution)/shard_map/all_to_all | solution.py:100
  310.5 5.5 all-to-all-start.1
  322.1 3.3 gather_fusion.4
  325.5 3.9 select_convert_fusion
  329.4 5.2 reshape.223
  334.5 41.2 %all-to-all-done.1 = bf16[16,36,2048]{2,1,0:T(8,128)(2,1)} async-done(((bf16[16,36,2048]{2,1,0:T(8,128)(2,1)}), bf16[16,36,2048]{2,1,0:T(8,128)(2,1)}, u32[]{:S(2)}, u32[]{:S(2)}) %all-to-all-start.1) | async-done | bytes 2359328 | tf_op jit(solution)/shard_map/all_to_all | solution.py:107
  378.4 3.3 gather_fusion.2
  381.7 3.9 select_convert_fusion.1
  385.6 5.2 reshape.222
  390.8 9.0 %multiply_reduce_fusion = (f32[128,2048]{1,0:T(8,128)S(1)}, f32[128,2048]{1,0:T(8,128)S(1)}) fusion(f32[128,4,2048]{2,1,0:T(4,128)} %reshape.223, f32[128,4]{1,0:T(8,128)S(1)} %copy.45, f32[128,4,2048]{2,1,0:T(4,128)} %reshape.222, f32[128,4]{1,0:T(8,128)S(1)} %copy.35), kind=kLoop, calls=%fused_computation.16 | loop fusion | flops 3670016 | bytes 10489856 | tf_op jit(solution)/shard_map/reduce_sum | solution.py:27
  399.9 4.4 gather_fusion
  404.4 5.2 gather.13
  409.6 3.0 multiply_convert_fusion
  412.6 67.9 %all_to_all.25 = bf16[16,36,2048]{2,1,0:T(8,128)(2,1)S(1)} all-to-all(bf16[16,36,2048]{2,1,0:T(8,128)(2,1)S(1)} %multiply_convert_fusion), channel_id=1, replica_groups=mesh['dp'=16,'expert'=16] {'expert'}, dimensions={0} | all-to-all | bytes 4718592 | tf_op jit(solution)/shard_map/all_to_all | solution.py:121
  486.4 89.7 %all-reduce.3.cloned.1.call-done = (f32[1,768,64]{1,2,0:T(8,128)}, f32[1,64,2048]{2,1,0:T(8,128)}) async-done(((f32[1,768,64]{1,2,0:T(8,128)}, f32[1,64,2048]{2,1,0:T(8,128)}), (f32[1,768,64]{1,2,0:T(8,128)}, f32[1,64,2048]{2,1,0:T(8,128)})) %all-reduce.3.cloned.1.call-update) | async-done | bytes 720912 | tf_op jit(solution)/shard_map/psum | solution.py:143
  (102 shorter events, 41.7 us)
Async XLA Ops:
  7.2 8.2 %copy-start = (bf16[128,2048]{1,0:T(8,128)(2,1)S(1)}, bf16[128,2048]{1,0:T(8,128)(2,1)}, u32[]{:S(2)}) copy-start(bf16[128,2048]{1,0:T(8,128)(2,1)} %param.14) | copy-start | bytes 1572868
  7.2 94.9 %all-gather.4.cloned.1.call-start = ((), (), s32[]{:S(2)}) async-start(), calls=%async_computation.5 | async-start | bytes 6684672 | tf_op jit(solution)/shard_map/all_gather | solution.py:66
  7.9 145.4 %all-gather.8.cloned.1.call-start = ((), (), s32[]{:S(2)}) async-start(), calls=%async_computation.7 | async-start | bytes 6684672 | tf_op jit(solution)/shard_map/all_gather | solution.py:68
  8.7 214.0 %all-gather.6.cloned.1.call-start = ((), (), s32[]{:S(2)}) async-start(), calls=%async_computation.6 | async-start | bytes 6684672 | tf_op jit(solution)/shard_map/all_gather | solution.py:67
  23.5 10.1 %copy-start.9 = (s32[128,4]{0,1:T(4,128)S(1)}, s32[128,4]{0,1:T(4,128)}, u32[]{:S(2)}) copy-start(s32[128,4]{0,1:T(4,128)} %param.16) | copy-start | bytes 6148
  23.5 69.7 %all-to-all-start.2 = ((bf16[16,36,2048]{2,1,0:T(8,128)(2,1)}), bf16[16,36,2048]{2,1,0:T(8,128)(2,1)S(1)}, u32[]{:S(2)}, u32[]{:S(2)}) async-start(bf16[16,36,2048]{2,1,0:T(8,128)(2,1)} %reshape.217), calls=%async_computation.2 | async-start | bytes 5242880 | tf_op jit(solution)/shard_map/all_to_all | solution.py:63
  93.2 148.4 %all-to-all-start = ((bf16[16,36,2048]{2,1,0:T(8,128)(2,1)}), bf16[16,36,2048]{2,1,0:T(8,128)(2,1)}, u32[]{:S(2)}, u32[]{:S(2)}) async-start(bf16[16,36,2048]{2,1,0:T(8,128)(2,1)} %reshape.207), calls=%async_computation | async-start | bytes 5242880 | tf_op jit(solution)/shard_map/all_to_all | solution.py:64
  102.1 120.6 %copy-start.5 = (bf16[16,36,2048]{2,0,1:T(8,128)(2,1)S(1)}, bf16[16,36,2048]{2,0,1:T(8,128)(2,1)}, u32[]{:S(2)}) copy-start(bf16[16,36,2048]{2,0,1:T(8,128)(2,1)} %copy.40) | copy-start | bytes 7077892
  241.6 67.5 %all-to-all-start.3 = ((bf16[16,36,2048]{2,1,0:T(8,128)(2,1)}), bf16[16,36,2048]{2,1,0:T(8,128)(2,1)S(1)}, u32[]{:S(2)}, u32[]{:S(2)}) async-start(bf16[16,36,2048]{2,1,0:T(8,128)(2,1)} %copy.44), calls=%async_computation.3 | async-start | bytes 5242880 | tf_op jit(solution)/shard_map/all_to_all | solution.py:100
  249.4 11.2 %slice-start = ((s8[6291456]{0:T(1024)(128)(4,1)}), s8[4194304]{0:T(1024)(128)(4,1)S(1)}, s32[]{:S(2)}) async-start(s8[6291456]{0:T(1024)(128)(4,1)} %bitcast.160), calls=%async_computation.9 | async-start | bytes 8388608
  254.5 5.2 copy-start.8
  254.5 6.1 %slice-start.1 = ((s8[6291456]{0:T(1024)(128)(4,1)}), s8[2097152]{0:T(1024)(128)(4,1)S(1)}, s32[]{:S(2)}) async-start(s8[6291456]{0:T(1024)(128)(4,1)} %bitcast.160), calls=%async_computation.10 | async-start | bytes 4194304
  259.7 3.2 copy-start.3
  260.6 2.3 copy-start.6
  268.8 47.4 %copy-start.10 = (f32[128,4]{0,1:T(4,128)S(1)}, f32[128,4]{0,1:T(4,128)}, u32[]{:S(2)}) copy-start(f32[128,4]{0,1:T(4,128)} %param.17) | copy-start | bytes 6148
  268.8 47.5 %copy-start.11 = (f32[128,4]{0,1:T(4,128)S(1)}, f32[128,4]{0,1:T(4,128)}, u32[]{:S(2)}) copy-start(f32[128,4]{0,1:T(4,128)} %param.18) | copy-start | bytes 6148
  309.0 1.5 copy-start.2
  310.5 65.2 %all-to-all-start.1 = ((bf16[16,36,2048]{2,1,0:T(8,128)(2,1)}), bf16[16,36,2048]{2,1,0:T(8,128)(2,1)}, u32[]{:S(2)}, u32[]{:S(2)}) async-start(bf16[16,36,2048]{2,1,0:T(8,128)(2,1)} %add_convert_fusion), calls=%async_computation.1 | async-start | bytes 5242880 | tf_op jit(solution)/shard_map/all_to_all | solution.py:107
  316.1 260.0 %all-reduce.3.cloned.1.call-start = ((), (), s32[]{:S(2)}) async-start(), calls=%async_computation.8 | async-start | bytes 1441792 | tf_op jit(solution)/shard_map/psum | solution.py:143
  412.6 67.9 %copy-start.7 = (f32[1,64,2048]{2,1,0:T(8,128)S(1)}, f32[1,64,2048]{2,1,0:T(8,128)}, u32[]{:S(2)}) copy-start(f32[1,64,2048]{2,1,0:T(8,128)} %param.23) | copy-start | bytes 1572868
  480.5 2.2 copy-start.4
  480.5 98.5 %copy-start.1 = (bf16[128,2048]{1,0:T(8,128)(2,1)S(1)}, bf16[128,2048]{1,0:T(8,128)(2,1)}, u32[]{:S(2)}) copy-start(bf16[128,2048]{1,0:T(8,128)(2,1)} %param.14) | copy-start | bytes 1572868
Sparse Core Ops, SparseCore 0:
  10.4 69.9 all-gather.3
  82.8 70.4 all-gather.7
  155.8 66.8 all-gather.5
  486.5 89.5 all-reduce.2
where the time goes:
time: 592 us; the launch traced here: 586 us
  waiting for transfers between devices  329 us (56%)
  local copies, waits for them, and re-layouts  69.7 us (12%)
  blocking collectives  67.9 us (11%)
  matrix products  46.3 us (8%)
  starting transfers between devices  29.9 us (5%)
  other arithmetic  28.7 us (5%)
  between operations  14.4 us (2%)
    psum x1, waiting for transfers between devices, shards(): sum_a, sum_b = lax.psum((part_a, part_b), 'dp')  89.7 us
    all_gather x1, waiting for transfers between devices, shards(): lax.all_gather(up_weight, 'dp', axis=1, tiled=True)  69.4 us
    all_to_all x1, blocking collectives, shards(): lax.all_to_all(grad_send.reshape(peers, resident_pruned_experts * cap_pru...  67.9 us
    all_to_all x1, waiting for transfers between devices, shards(): lax.all_to_all(frozen_send, 'expert', split_axis=0, concat_axis=0, tiled=...  43.5 us
    all_gather x1, waiting for transfers between devices, shards(): lax.all_gather(down_weight, 'dp', axis=2, tiled=True)  42.9 us
    all_to_all x1, waiting for transfers between devices, shards(): lax.all_to_all(pruned_out.reshape(peers, resident_pruned_experts * cap_pr...  41.2 us
    all_to_all x1, waiting for transfers between devices, shards(): lax.all_to_all(frozen_out.reshape(peers, local_experts * cap_frozen, widt...  40.2 us
    dot_general x1, matrix products, shards(): jnp.einsum('secf,efd->secd', frozen_hidden, down_full, preferred_element_...  12.9 us
  transfers between devices with their start and end apart: 8, of which 6 were waited for; matrix products, arithmetic and copies ran while one was open for 17% of the time, Pallas kernels for 0%

commit v1 on v0

v1 whole, which is shorter than its diff:
```python
import functools

import jax
import jax.numpy as jnp
from jax import lax
from jax.experimental import pallas as pl
from jax.experimental.pallas import tpu as pltpu
from jax.sharding import PartitionSpec as P

BF = jnp.bfloat16
F32 = jnp.float32
MESH = pl.DeviceIdType.MESH
ANY = pl.BlockSpec(memory_space=pl.ANY)
VM = pl.BlockSpec(memory_space=pltpu.VMEM)

NX = 4
NZ = 8
GROUP = 16
BLOCK = 128
WIDTH = 2048
HIDDEN = 768
RANK = 64
QUADS = 4
TOKQ = 4 * BLOCK
CAPF = 18
CAPP = 36
RF = 80
RP = 144
RQ = 2 * RF + RP
ROWS0 = QUADS * (RF + RP)
ROWS1 = QUADS * RF
CHUNK = 256


class Place:
    def __init__(self):
        dp, ex = lax.axis_index("dp"), lax.axis_index("expert")
        self.dp, self.ex = dp, ex
        self.x, self.y = lax.rem(dp, NX), lax.div(dp, NX)
        self.z, self.c = lax.div(ex, 2), lax.rem(ex, 2)

    def xy(self, dx, dy):
        return lax.rem(self.y + dy + NX, NX) * NX + lax.rem(self.x + dx + NX, NX)

    def zz(self, dz):
        return lax.rem(self.z + dz + NZ, NZ)

    def dev_xy(self, dx, dy):
        return (self.xy(dx, dy), self.ex)

    def dev_z(self, dz):
        return (self.dp, self.zz(dz) * 2 + self.c)

    def partner(self):
        return (self.dp, self.z * 2 + 1 - self.c)


def barrier(devices):
    sem = pltpu.get_barrier_semaphore()
    for d in devices:
        pl.semaphore_signal(sem, inc=1, device_id=d, device_id_type=MESH)
    pl.semaphore_wait(sem, len(devices))


class Sender:
    def __init__(self, send_sem, recv_sem):
        self.send_sem, self.recv_sem = send_sem, recv_sem
        self.count = 0
        self.sent = []

    def send(self, src, dst, device):
        n = self.count
        self.count += 1
        cp = pltpu.make_async_remote_copy(
            src_ref=src, dst_ref=dst, send_sem=self.send_sem.at[n], recv_sem=self.recv_sem.at[n],
            device_id=device, device_id_type=MESH,
        )
        cp.start()
        self.sent.append(cp)
        return n

    def arrived(self, n, region, device):
        pltpu.make_async_remote_copy(
            src_ref=region, dst_ref=region, send_sem=self.send_sem.at[n], recv_sem=self.recv_sem.at[n],
            device_id=device, device_id_type=MESH,
        ).wait_recv()

    def finish(self):
        for cp in self.sent:
            cp.wait_send()


def gather_z(me, tx, own, region):
    c = me.c
    half = own.shape[0] // 2

    def part(ref, h):
        return ref if h is None else ref.at[pl.ds(h * half, half)]

    plus = tx.send(own, region(me.z, c, None), me.dev_z(1))
    minus = tx.send(own, region(me.z, c, None), me.dev_z(-1))
    got = [(tx.send(own, region(me.z, c, None), me.partner()), 0, None)]
    yield
    for k in (1, 2, 3):
        zl, zr = me.zz(-k), me.zz(k)
        tx.arrived(plus, region(zl, c, None), me.dev_z(1))
        plus = (tx.send(region(zl, c, None), region(zl, c, None), me.dev_z(1)) if k < 3
                else tx.send(region(zl, c, 0), region(zl, c, 0), me.dev_z(1)))
        got.append((tx.send(region(zl, c, None), region(zl, c, None), me.partner()), -k, None))
        tx.arrived(minus, region(zr, c, None), me.dev_z(-1))
        minus = (tx.send(region(zr, c, None), region(zr, c, None), me.dev_z(-1)) if k < 3
                 else tx.send(region(zr, c, 1), region(zr, c, 1), me.dev_z(-1)))
        got.append((tx.send(region(zr, c, None), region(zr, c, None), me.partner()), k, None))
        yield
    zo = me.zz(4)
    tx.arrived(plus, region(zo, c, 0), me.dev_z(1))
    got.append((tx.send(region(zo, c, 0), region(zo, c, 0), me.partner()), 4, 0))
    tx.arrived(minus, region(zo, c, 1), me.dev_z(-1))
    got.append((tx.send(region(zo, c, 1), region(zo, c, 1), me.partner()), 4, 1))
    yield
    for n, k, h in got:
        tx.arrived(n, region(me.zz(k), 1 - c, h), me.partner())
    yield


def gather_xy(me, tx, own, region, x_first):
    def at(p, q):
        return (p, q) if x_first else (q, p)

    def idx(p, q):
        return me.xy(*at(p, q))

    def dev(p, q):
        return me.dev_xy(*at(p, q))

    def src(p, q, h):
        return own(h) if (p, q) == (0, 0) else region(idx(p, q), h)

    def ring(p, q, along):
        dp_, dq_ = (1, 0) if along == "p" else (0, 1)
        a = tx.send(src(p, q, None), region(idx(p, q), None), dev(dp_, dq_))
        b = tx.send(src(p, q, None), region(idx(p, q), None), dev(-dp_, -dq_))
        return a, b

    first = ring(0, 0, "p")
    second = {0: ring(0, 0, "q")}
    yield
    tx.arrived(first[0], region(idx(-1, 0), None), dev(1, 0))
    o0 = tx.send(region(idx(-1, 0), 0), region(idx(-1, 0), 0), dev(1, 0))
    second[-1] = ring(-1, 0, "q")
    tx.arrived(first[1], region(idx(1, 0), None), dev(-1, 0))
    o1 = tx.send(region(idx(1, 0), 1), region(idx(1, 0), 1), dev(-1, 0))
    second[1] = ring(1, 0, "q")
    yield
    tx.arrived(o0, region(idx(2, 0), 0), dev(1, 0))
    tx.arrived(o1, region(idx(2, 0), 1), dev(-1, 0))
    second[2] = ring(2, 0, "q")
    yield
    last = []
    for p in (0, -1, 1, 2):
        a, b = second[p]
        tx.arrived(a, region(idx(p, -1), None), dev(0, 1))
        last.append((tx.send(region(idx(p, -1), 0), region(idx(p, -1), 0), dev(0, 1)), p, 0))
        tx.arrived(b, region(idx(p, 1), None), dev(0, -1))
        last.append((tx.send(region(idx(p, 1), 1), region(idx(p, 1), 1), dev(0, -1)), p, 1))
        if p == -1:
            yield
    yield
    for n, p, h in last:
        tx.arrived(n, region(idx(p, 2), h), dev(0, 1))
    yield


SENDS1 = 6 * 20 + 2 * 17


def collect_kernel(gate, up, down, tok, meta, gate_o, up_o, down_o, tok_o, meta_o,
                   st_g, st_u, st_d, st_t, st_m, send_sem, recv_sem, loc_sem):
    me = Place()
    tx = Sender(send_sem, recv_sem)
    stage = ((gate, st_g), (up, st_u), (down, st_d), (tok, st_t), (meta, st_m))
    loads = [pltpu.make_async_copy(a, b, loc_sem.at[i]) for i, (a, b) in enumerate(stage)]
    for cp in loads:
        cp.start()
    barrier([me.dev_xy(1, 0), me.dev_xy(-1, 0), me.dev_xy(0, 1), me.dev_xy(0, -1),
             me.dev_z(1), me.dev_z(-1), me.partner()])

    def block_region(ref, size):
        def region(z, c, h):
            v = ref.at[z * 2 + c]
            return v if h is None else v.at[pl.ds(h * (size // 2), size // 2)]
        return region

    def rows_region(ref, e):
        n = WIDTH // GROUP

        def region(dp, h):
            if h is None:
                return ref.at[e, pl.ds(pl.multiple_of(dp * n, n), n), :]
            return ref.at[e, pl.ds(pl.multiple_of(dp * n + h * (n // 2), n // 2), n // 2), :]
        return region

    def cols_region(ref, e):
        n = WIDTH // GROUP

        def region(dp, h):
            cols = pl.ds(pl.multiple_of(dp * n, n), n)
            if h is None:
                return ref.at[e, :, cols]
            return ref.at[e, pl.ds(h * (HIDDEN // 2), HIDDEN // 2), cols]
        return region

    def own_half(ref, e):
        def own(h):
            v = ref.at[e]
            n = v.shape[0] // 2
            return v if h is None else v.at[pl.ds(h * n, n)]
        return own

    def jobs(ref, region_of, out):
        return [gather_xy(me, tx, own_half(ref, e), region_of(out, e), e == 0) for e in (0, 1)]

    meta_j = gather_z(me, tx, meta, block_region(meta_o, 16))
    tok_j = gather_z(me, tx, tok, block_region(tok_o, BLOCK))
    w_j = [jobs(gate, rows_region, gate_o), jobs(up, rows_region, up_o), jobs(down, cols_region, down_o)]

    def step(js):
        for j in js:
            next(j, None)

    step([meta_j])
    step(w_j[0])
    step([tok_j])
    step(w_j[1])
    outs = (gate_o.at[:, pl.ds(pl.multiple_of(me.dp * BLOCK, BLOCK), BLOCK), :],
            up_o.at[:, pl.ds(pl.multiple_of(me.dp * BLOCK, BLOCK), BLOCK), :],
            down_o.at[:, :, pl.ds(pl.multiple_of(me.dp * BLOCK, BLOCK), BLOCK)],
            tok_o.at[me.ex], meta_o.at[me.ex])
    stores = []
    for i, cp in enumerate(loads):
        cp.wait()
        stores.append(pltpu.make_async_copy(stage[i][1], outs[i], loc_sem.at[5 + i]))
        stores[-1].start()
    step(w_j[2])
    for _ in range(8):
        step(w_j[0])
        step([meta_j, tok_j])
        step(w_j[1])
        step(w_j[2])
    for cp in stores:
        cp.wait()
    tx.finish()


def collect(gate, up, down, tok, meta):
    sds = jax.ShapeDtypeStruct
    return pl.pallas_call(
        collect_kernel,
        out_shape=(sds((2, WIDTH, HIDDEN), BF), sds((2, WIDTH, HIDDEN), BF), sds((2, HIDDEN, WIDTH), BF),
                   sds((GROUP, BLOCK, WIDTH), BF), sds((GROUP, 16, BLOCK), F32)),
        in_specs=[ANY] * 5,
        out_specs=(ANY,) * 5,
        scratch_shapes=[pltpu.VMEM(a.shape, a.dtype) for a in (gate, up, down, tok, meta)]
        + [pltpu.SemaphoreType.DMA((SENDS1,)), pltpu.SemaphoreType.DMA((SENDS1,)), pltpu.SemaphoreType.DMA((10,))],
        compiler_params=pltpu.CompilerParams(collective_id=0, has_side_effects=True),
        name="collect",
    )(gate, up, down, tok, meta)


def split2(v):
    hi = v.astype(BF)
    return hi, (v - hi.astype(F32)).astype(BF)


def dot(a, b):
    return jnp.dot(a, b, preferred_element_type=F32)


def tables(meta):
    ex = lax.axis_index("expert").astype(F32)
    row = lax.broadcasted_iota(jnp.int32, (BLOCK, BLOCK), 0)
    col = lax.broadcasted_iota(jnp.int32, (BLOCK, BLOCK), 1)
    before = (row < col).astype(BF)
    quarter = lax.rem(lax.broadcasted_iota(jnp.int32, (GROUP, BLOCK), 0), 4).astype(F32)

    def one(ids, shares, which, cap):
        hit = (ids == which).astype(F32)
        named = jnp.sum(hit, axis=1)
        share = jnp.sum(hit * shares, axis=1)
        pos = dot(named.astype(BF), before) + quarter * cap
        return jnp.where(named > 0, pos, -1.0), share

    fid, pid, fsh, psh = (meta[:, 4 * i:4 * i + 4, :] for i in range(4))
    a = one(fid, fsh, 2.0 * ex, CAPF)
    b = one(fid, fsh, 2.0 * ex + 1.0, CAPF)
    p = one(pid, psh, ex, CAPP)
    return a, b, p


def quad_row(v, q):
    return jnp.concatenate([v[4 * q + i:4 * q + i + 1, :] for i in range(4)], axis=1)


def quad_col(v, first, q):
    return jnp.concatenate([v[:, first + 4 * q + i:first + 4 * q + i + 1] for i in range(4)], axis=0)


def pick(rows, pos):
    slot = lax.broadcasted_iota(jnp.int32, (rows, TOKQ), 0).astype(F32)
    return (slot == pos).astype(BF)


def put(rows, pos, share):
    slot = lax.broadcasted_iota(jnp.int32, (TOKQ, rows), 1).astype(F32)
    return jnp.where(slot == pos, share, 0.0)


def experts_kernel(gate_h, up_h, down_h, tok_h, meta, first, second, part_h, hid_o, low_o,
                   gate, up, down, tok, x0, x1, h0, h1, wt, low3, b3, rows, outb, sems, out_sem):
    loads = []
    for q in range(QUADS):
        loads.append(pltpu.make_async_copy(tok_h.at[pl.ds(4 * q, 4)], tok.at[pl.ds(4 * q, 4)], sems.at[q]))
    for i, (s, d) in enumerate(((gate_h, gate), (up_h, up), (down_h, down))):
        loads.append(pltpu.make_async_copy(s, d, sems.at[QUADS + i]))
    for cp in loads:
        cp.start()

    (pa, wa), (pb, wb), (pp, wp) = tables(meta[...])
    cols = jnp.transpose(jnp.concatenate([pa, pb, pp, -wa, -wb, wp, pp, wp], axis=0))
    for q in range(QUADS):
        wt[q] = jnp.concatenate([
            put(RF, quad_col(cols, 0, q), quad_col(cols, 48, q)),
            put(RP, quad_col(cols, 32, q), quad_col(cols, 80, q)),
            put(RF, quad_col(cols, 16, q), quad_col(cols, 64, q)),
        ], axis=1).astype(BF)
    bh, bl = split2(second[0])
    b3[0:RANK], b3[RANK:2 * RANK], b3[2 * RANK:] = bh, bh, bl

    for q in range(QUADS):
        loads[q].wait()
        oa, op, ob = pick(RF, quad_row(pa, q)), pick(RP, quad_row(pp, q)), pick(RF, quad_row(pb, q))

        def gather(i, _):
            at = pl.ds(pl.multiple_of(i * 512, 512), 512)
            t = tok[4 * q:4 * q + 4, :, at].reshape(TOKQ, 512)
            x0[q * RF:(q + 1) * RF, at] = dot(oa, t).astype(BF)
            x0[QUADS * RF + q * RP:QUADS * RF + (q + 1) * RP, at] = dot(op, t).astype(BF)
            x1[q * RF:(q + 1) * RF, at] = dot(ob, t).astype(BF)
            return 0

        lax.fori_loop(0, 4, gather, 0)

    loads[QUADS].wait()
    loads[QUADS + 1].wait()

    def hidden(x, h, e, m, n):
        rows_m = x.shape[0] // m

        def body(i, _):
            rr = pl.ds(pl.multiple_of(lax.rem(i, m) * rows_m, rows_m), rows_m)
            cc = pl.ds(pl.multiple_of(lax.div(i, m) * n, n), n)
            g = dot(x[rr, :], gate[e, :, cc])
            u = dot(x[rr, :], up[e, :, cc])
            h[rr, cc] = (g / (1.0 + jnp.exp(-g)) * u).astype(BF)
            return 0

        lax.fori_loop(0, m * (HIDDEN // n), body, 0)

    hidden(x0, h0, 0, 2, CHUNK)
    hidden(x1, h1, 1, 1, CHUNK)

    hid = h0[QUADS * RF:, :]
    ah, al = split2(first[0])
    low2 = dot(hid, jnp.concatenate([ah, al], axis=1))
    low = low2[:, :RANK] + low2[:, RANK:]
    lh, ll = split2(low)
    low3[...] = jnp.concatenate([lh, ll, lh], axis=1)
    hid_o[...] = hid
    low_o[...] = low
    loads[QUADS + 2].wait()

    def out_copy(i, slot):
        at = pl.ds(pl.multiple_of(i * CHUNK, CHUNK), CHUNK)
        return pltpu.make_async_copy(outb.at[slot], part_h.at[:, at], out_sem.at[slot])

    def down_step(i, _):
        at = pl.ds(pl.multiple_of(i * CHUNK, CHUNK), CHUNK)
        slot = lax.rem(i, 2)
        r0 = dot(h0[...], down[0, :, at])
        rp = r0[QUADS * RF:] + dot(low3[...], b3[:, at])
        r1 = dot(h1[...], down[1, :, at])
        for q in range(QUADS):
            rows[q, 0:RF] = r0[q * RF:(q + 1) * RF].astype(BF)
            rows[q, RF:RF + RP] = rp[q * RP:(q + 1) * RP].astype(BF)
            rows[q, RF + RP:] = r1[q * RF:(q + 1) * RF].astype(BF)

        @pl.when(i >= 2)
        def _():
            out_copy(i - 2, slot).wait()

        for q in range(QUADS):
            outb[slot, q * TOKQ:(q + 1) * TOKQ, :] = dot(wt[q], rows[q]).astype(BF)
        out_copy(i, slot).start()
        return 0

    steps = WIDTH // CHUNK
    lax.fori_loop(0, steps, down_step, 0)
    for i in (steps - 2, steps - 1):
        out_copy(i, i % 2).wait()


def experts(gate, up, down, tok, meta, first, second):
    sds = jax.ShapeDtypeStruct
    vm = pltpu.VMEM
    return pl.pallas_call(
        experts_kernel,
        out_shape=(sds((GROUP * BLOCK, WIDTH), BF), sds((QUADS * RP, HIDDEN), BF), sds((QUADS * RP, RANK), F32)),
        in_specs=[ANY] * 4 + [VM] * 3,
        out_specs=(ANY, VM, VM),
        scratch_shapes=[
            vm(gate.shape, BF), vm(up.shape, BF), vm(down.shape, BF), vm(tok.shape, BF),
            vm((ROWS0, WIDTH), BF), vm((ROWS1, WIDTH), BF), vm((ROWS0, HIDDEN), BF), vm((ROWS1, HIDDEN), BF),
            vm((QUADS, TOKQ, RQ), BF), vm((QUADS * RP, 3 * RANK), BF), vm((3 * RANK, WIDTH), BF),
            vm((QUADS, RQ, CHUNK), BF), vm((2, GROUP * BLOCK, CHUNK), BF),
            pltpu.SemaphoreType.DMA((QUADS + 3,)), pltpu.SemaphoreType.DMA((2,)),
        ],
        compiler_params=pltpu.CompilerParams(vmem_limit_bytes=60 << 20),
        name="experts",
    )(gate, up, down, tok, meta, first, second)


SENDS3 = 8 + 14 + 17


def reduce_kernel(part, out, mine, theirs, ring, own, send_sem, recv_sem, loc_sem):
    me = Place()
    tx = Sender(send_sem, recv_sem)
    half = BLOCK // 2
    order = (4, 3, -3, 2, -2, 1, -1, 0)
    loads = {}
    for i, k in enumerate(order):
        loads[k] = pltpu.make_async_copy(part.at[me.zz(k) * 2 + me.c], mine.at[me.zz(k)], loc_sem.at[i])
        loads[k].start()
    barrier([me.dev_z(1), me.dev_z(-1), me.partner()])
    swap = {}
    for k in order:
        swap[k] = tx.send(part.at[me.zz(k) * 2 + 1 - me.c], theirs.at[me.zz(k)], me.partner())

    def pair_sum(k):
        loads[k].wait()
        tx.arrived(swap[k], theirs.at[me.zz(k)], me.partner())
        d = me.zz(k)
        mine[d] = (mine[d].astype(F32) + theirs[d].astype(F32)).astype(BF)

    def rows(h):
        return pl.ds(h * half, half)

    slot = {}
    waiting = {}

    def push(sign, h, j):
        d = me.zz(sign * j)
        key = (sign, h)
        if key in waiting:
            n, s = waiting[key]
            tx.arrived(n, ring.at[s], me.dev_z(sign))
            mine[d, rows(h)] = (mine[d, rows(h)].astype(F32) + ring[s].astype(F32)).astype(BF)
        s = slot.setdefault((sign, h, j), len(slot))
        waiting[key] = (tx.send(mine.at[d, rows(h)], ring.at[s], me.dev_z(sign)), s)

    pair_sum(4)
    push(1, 0, 4)
    push(-1, 1, 4)
    for j in (3, 2, 1):
        pair_sum(j)
        pair_sum(-j)
        push(1, 1, j)
        push(-1, 0, j)
        push(1, 0, j)
        push(-1, 1, j)
    pair_sum(0)
    for h in (1, 0):
        total = mine[me.z, rows(h)].astype(F32)
        for sign in (1, -1):
            n, s = waiting[(sign, h)]
            tx.arrived(n, ring.at[s], me.dev_z(sign))
            total = total + ring[s].astype(F32)
        own[rows(h)] = total.astype(BF)

    def region(z, c, h):
        v = out.at[z * 2 + c]
        return v if h is None else v.at[rows(h)]

    last = pltpu.make_async_copy(own, out.at[me.ex], loc_sem.at[8])
    last.start()
    for _ in gather_z(me, tx, own, region):
        pass
    last.wait()
    tx.finish()


def reduce_residual(part):
    vm = pltpu.VMEM
    return pl.pallas_call(
        reduce_kernel,
        out_shape=jax.ShapeDtypeStruct((GROUP, BLOCK, WIDTH), BF),
        in_specs=[ANY],
        out_specs=ANY,
        scratch_shapes=[
            vm((NZ, BLOCK, WIDTH), BF), vm((NZ, BLOCK, WIDTH), BF), vm((14, BLOCK // 2, WIDTH), BF),
            vm((BLOCK, WIDTH), BF),
            pltpu.SemaphoreType.DMA((SENDS3,)), pltpu.SemaphoreType.DMA((SENDS3,)), pltpu.SemaphoreType.DMA((9,)),
        ],
        compiler_params=pltpu.CompilerParams(collective_id=1, has_side_effects=True),
        name="reduce_residual",
    )(part)


def grads_kernel(res_h, meta, hid, low, second, ga_o, gb_o, res, back, sems):
    loads = []
    for q in range(QUADS):
        loads.append(pltpu.make_async_copy(res_h.at[pl.ds(4 * q, 4)], res.at[pl.ds(4 * q, 4)], sems.at[q]))
    for cp in loads:
        cp.start()
    (_, _), (_, _), (pp, wp) = tables(meta[...])
    bh, bl = split2(second[0])
    b2 = jnp.concatenate([bh, bl], axis=0)
    nt = (((1,), (1,)), ((), ()))
    tn = (((0,), (0,)), ((), ()))
    gb = jnp.zeros((2 * RANK, WIDTH), F32)
    for q in range(QUADS):
        op = pick(RP, quad_row(pp, q))
        share = quad_row(wp, q)
        lq = low[q * RP:(q + 1) * RP, :]
        l1 = lq.astype(BF)
        r1 = lq - l1.astype(F32)
        l2 = r1.astype(BF)
        l3 = (r1 - l2.astype(F32)).astype(BF)
        spread = lax.dot_general(jnp.concatenate([l1, l2, l3, jnp.zeros_like(l1)], axis=1), op, tn,
                                 preferred_element_type=F32)
        low_t = (spread[0:RANK] + spread[RANK:2 * RANK] + spread[2 * RANK:3 * RANK]) * share
        th, tl = split2(low_t)
        loads[q].wait()
        rq = res[4 * q:4 * q + 4].reshape(TOKQ, WIDTH)
        gb = gb + dot(jnp.concatenate([th, tl], axis=0), rq)
        bt = lax.dot_general(b2, rq, nt, preferred_element_type=F32)
        bt = (bt[:RANK] + bt[RANK:]) * share
        b_hi, b_lo = split2(bt)
        picked = lax.dot_general(op, jnp.concatenate([b_hi, b_lo], axis=0), nt, preferred_element_type=F32)
        back[q * RP:(q + 1) * RP, :] = picked.astype(BF)
    gb_o[...] = gb[:RANK] + gb[RANK:]
    ga = lax.dot_general(hid[...], back[...], tn, preferred_element_type=F32)
    ga_o[...] = ga[:, :RANK] + ga[:, RANK:]


def grads(res, meta, hid, low, second):
    sds = jax.ShapeDtypeStruct
    vm = pltpu.VMEM
    return pl.pallas_call(
        grads_kernel,
        out_shape=(sds((HIDDEN, RANK), F32), sds((RANK, WIDTH), F32)),
        in_specs=[ANY] + [VM] * 4,
        out_specs=(VM, VM),
        scratch_shapes=[vm((GROUP, BLOCK, WIDTH), BF), vm((QUADS * RP, 2 * RANK), BF), pltpu.SemaphoreType.DMA((QUADS,))],
        compiler_params=pltpu.CompilerParams(vmem_limit_bytes=60 << 20),
        name="grads",
    )(res, meta, hid, low, second)


def exchange_kernel(pa, pb, ga, gb, ra, rb, send_sem, recv_sem):
    dp, ex = lax.axis_index("dp"), lax.axis_index("expert")
    tx = Sender(send_sem, recv_sem)
    na, nb = HIDDEN // GROUP, WIDTH // GROUP

    def dev(o):
        return (lax.rem(dp + o, GROUP), ex)

    barrier([dev(o) for o in range(1, GROUP)])
    got = []
    for o in range(1, GROUP):
        d = lax.rem(dp + o, GROUP)
        got.append(tx.send(pa.at[pl.ds(pl.multiple_of(d * na, na), na)], ra.at[o - 1], dev(o)))
        got.append(tx.send(pb.at[:, pl.ds(pl.multiple_of(d * nb, nb), nb)], rb.at[o - 1], dev(o)))
    ta = pa[pl.ds(pl.multiple_of(dp * na, na), na), :]
    tb = pb[:, pl.ds(pl.multiple_of(dp * nb, nb), nb)]
    for o in range(1, GROUP):
        tx.arrived(got[2 * o - 2], ra.at[o - 1], dev(o))
        tx.arrived(got[2 * o - 1], rb.at[o - 1], dev(o))
        ta = ta + ra[o - 1]
        tb = tb + rb[o - 1]
    ga[...] = ta
    gb[...] = tb
    tx.finish()


def exchange(pa, pb):
    sds = jax.ShapeDtypeStruct
    vm = pltpu.VMEM
    na, nb = HIDDEN // GROUP, WIDTH // GROUP
    n = 2 * (GROUP - 1)
    return pl.pallas_call(
        exchange_kernel,
        out_shape=(sds((na, RANK), F32), sds((RANK, nb), F32)),
        in_specs=[VM, VM],
        out_specs=(VM, VM),
        scratch_shapes=[
            vm((GROUP - 1, na, RANK), F32), vm((GROUP - 1, RANK, nb), F32),
            pltpu.SemaphoreType.DMA((n,)), pltpu.SemaphoreType.DMA((n,)),
        ],
        compiler_params=pltpu.CompilerParams(collective_id=2, has_side_effects=True),
        name="exchange",
    )(pa, pb)


def shards(tokens, fid, pid, fsc, psc, gate, up, down, first, second):
    fsh = fsc / jnp.sum(fsc, axis=1, keepdims=True)
    psh = psc / jnp.sum(psc, axis=1, keepdims=True)
    meta = jnp.concatenate([fid.astype(F32), pid.astype(F32), fsh, psh], axis=1).T
    gate_f, up_f, down_f, tok_f, meta_f = collect(gate, up, down, tokens, meta)
    part, hid, low = experts(gate_f, up_f, down_f, tok_f, meta_f, first, second)
    res = reduce_residual(part.reshape(GROUP, BLOCK, WIDTH))
    pa, pb = grads(res, meta_f, hid, low, second)
    ga, gb = exchange(pa, pb)
    return ga[None], gb[None]


def solution(mesh):
    rows = P(("dp", "expert"), None)
    return jax.shard_map(
        shards,
        mesh=mesh,
        in_specs=(rows,) * 5 + (P("expert", "dp", None), P("expert", "dp", None), P("expert", None, "dp"),
                                P("expert", None, None), P("expert", None, None)),
        out_specs=(P("expert", "dp", None), P("expert", None, "dp")),
        check_vma=False,
    )
```

time: 592 us -> 280 us (0.47)
  waiting for transfers between devices: 329 us -> 0 us
  Pallas kernels: 0 us -> 270 us
  blocking collectives: 67.9 us -> 0 us
  local copies, waits for them, and re-layouts: 69.7 us -> 4.56 us
  matrix products: 46.3 us -> 0 us
  starting transfers between devices: 29.9 us -> 0 us
  other arithmetic: 28.7 us -> 4.08 us
  between operations: 14.4 us -> 0.67 us
    pallas_call x0 -> x5, Pallas kernels: none -> 270 us  [the longest x1 108 us: collect(): pl.pallas_call(collect_kernel, out_shape=(sds((2, WIDTH, HIDDEN), BF), sd...]
    all_to_all x4 -> x0, waiting for transfers between devices: 125 us -> none  [the longest x1 43.5 us: shards(): lax.all_to_all(frozen_send, 'expert', split_axis=0, concat_axis=0, tiled=...]
    all_gather x3 -> x0, waiting for transfers between devices: 112 us -> none  [the longest x1 69.4 us: shards(): lax.all_gather(up_weight, 'dp', axis=1, tiled=True)]
    psum x1 -> x0, waiting for transfers between devices: 89.7 us -> none  [shards(): sum_a, sum_b = lax.psum((part_a, part_b), 'dp')]
    all_to_all x1 -> x0, blocking collectives: 67.9 us -> none  [shards(): lax.all_to_all(grad_send.reshape(peers, resident_pruned_experts * cap_pru...]
    dot_general x10 -> x0, matrix products: 46.3 us -> none  [the longest x1 12.9 us: shards(): jnp.einsum('secf,efd->secd', frozen_hidden, down_full, preferred_element_...]
    all_to_all x4 -> x0, starting transfers between devices: 29.7 us -> none  [the longest x1 10.1 us: shards(): lax.all_to_all(frozen_send, 'expert', split_axis=0, concat_axis=0, tiled=...]
    gather x6 -> x0, local copies, waits for them, and re-layouts: 24.3 us -> none  [the longest x2 9.64 us: shards(): jnp.take(residual, pruned_token_rows, axis=0) * pruned_gate_weights[:, None]]
  transfers between devices with their start and end apart: 8 -> 0, of which waited for: 6 -> 0; matrix products, arithmetic and copies ran while one was open for 17% -> 0% of each run, Pallas kernels for 0% -> 0%
where the time goes in v1:
time: 280 us; the launch traced here: 279 us
  Pallas kernels  270 us (96%)
  local copies, waits for them, and re-layouts  4.56 us (2%)
  other arithmetic  4.08 us (1%)
    pallas_call x1, Pallas kernels, collect(): pl.pallas_call(collect_kernel, out_shape=(sds((2, WIDTH, HIDDEN), BF), sd...  108 us
    pallas_call x1, Pallas kernels, reduce_residual(): pl.pallas_call(reduce_kernel, out_shape=jax.ShapeDtypeStruct((GROUP, BLOC...  96.3 us
    pallas_call x1, Pallas kernels, experts(): pl.pallas_call(experts_kernel, out_shape=(sds((GROUP * BLOCK, WIDTH), BF)...  38 us
    pallas_call x1, Pallas kernels, exchange(): pl.pallas_call(exchange_kernel, out_shape=(sds((na, RANK), F32), sds((RAN...  18.3 us
    pallas_call x1, Pallas kernels, grads(): pl.pallas_call(grads_kernel, out_shape=(sds((HIDDEN, RANK), F32), sds((RA...  9.76 us

profile of v1, /device:TPU:1, one launch (start us, length us, event | category | flops | bytes accessed | tf_op | source)
XLA Modules:
  0.0 279.2 jit_solution(13923788933958402828)
XLA Ops:
  0.6 0.7 reduce_sum.18
  1.3 0.7 reduce_sum.19
  2.0 0.7 convert_element_type.6
  2.7 0.7 convert_element_type.7
  3.4 0.7 broadcast_divide_fusion
  4.1 0.6 maximum_bitcast_fusion.meta
  4.7 1.8 copy.12.first
  6.5 107.5 %collect.1 = (bf16[2,2048,768]{2,1,0:T(8,128)(2,1)}, bf16[2,2048,768]{2,1,0:T(8,128)(2,1)}, bf16[2,768,2048]{2,1,0:T(8,128)(2,1)}, bf16[16,128,2048]{2,1,0:T(8,128)(2,1)}, f32[16,16,128]{2,1,0:T(8,128)}) custom-call(bf16[2,128,768]{2,1,0:T(8,128)(2,1)} %gate.1, bf16[2,128,768]{2,1,0:T(8,128)(2,1)} %up.1, bf16[2,768,128]{2,1,0:T(8,128)(2,1)} %down.1, ...), custom_call_target="tpu_custom_call" | custom-call | tf_op jit(solution)/shard_map/collect/pallas_call | solution.py:257
  114.1 38.0 %experts.1 = (bf16[2048,2048]{1,0:T(8,128)(2,1)}, bf16[576,768]{1,0:T(8,128)(2,1)}, f32[576,64]{1,0:T(8,128)}) custom-call(bf16[2,2048,768]{2,1,0:T(8,128)(2,1)} %get-tuple-element.14.gate_h, bf16[2,2048,768]{2,1,0:T(8,128)(2,1)} %get-tuple-element.15.up_h, bf16[2,768,2048]{2,1,0:T(8,128)(2,1)} %get-tuple-element.16.down_h, ...), custom_call_target="tpu_custom_call" | custom-call | tf_op jit(solution)/shard_map/experts/pallas_call | solution.py:415
  152.1 96.3 %reduce_residual.1.res_h = bf16[16,128,2048]{2,1,0:T(8,128)(2,1)} custom-call(bf16[16,128,2048]{2,1,0:T(8,128)(2,1)} %bitcast.5), custom_call_target="tpu_custom_call" | custom-call | tf_op jit(solution)/shard_map/reduce_residual/pallas_call | solution.py:504
  248.4 9.8 %grads.1 = (f32[768,64]{1,0:T(8,128)}, f32[64,2048]{1,0:T(8,128)}) custom-call(bf16[16,128,2048]{2,1,0:T(8,128)(2,1)} %reduce_residual.1.res_h, f32[16,16,128]{2,1,0:T(8,128)} %get-tuple-element.18.meta, bf16[576,768]{1,0:T(8,128)(2,1)} %get-tuple-element.20.hid, f32[576,64]{1,0:T(8,128)} %get-tuple-element.21.low, f32[1,64,2048]{2,1,0:T(8,128)} %second.3), custom_call_target="tpu_custom_call" | custom-call | tf_op jit(solution)/shard_map/grads/pallas_call | solution.py:559
  258.2 18.3 %exchange.1 = (f32[48,64]{1,0:T(8,128)}, f32[64,128]{1,0:T(8,128)}) custom-call(f32[768,64]{1,0:T(8,128)} %get-tuple-element.22.pa, f32[64,2048]{1,0:T(8,128)} %get-tuple-element.23.pb), custom_call_target="tpu_custom_call" | custom-call | tf_op jit(solution)/shard_map/exchange/pallas_call | solution.py:601
  276.5 1.3 copy.15
  277.8 1.4 copy.16

commit v2 on v1

v2 whole, which is shorter than its diff:
```python
import functools

import jax
import jax.numpy as jnp
from jax import lax
from jax.experimental import pallas as pl
from jax.experimental.pallas import tpu as pltpu
from jax.sharding import PartitionSpec as P

BF = jnp.bfloat16
F32 = jnp.float32
MESH = pl.DeviceIdType.MESH
ANY = pl.BlockSpec(memory_space=pl.ANY)
VM = pl.BlockSpec(memory_space=pltpu.VMEM)

NX = 4
NZ = 8
GROUP = 16
BLOCK = 128
WIDTH = 2048
HIDDEN = 768
RANK = 64
QUADS = 4
TOKQ = 4 * BLOCK
CAPF = 18
CAPP = 36
RF = 80
RP = 144
RQ = 2 * RF + RP
ROWS0 = QUADS * (RF + RP)
ROWS1 = QUADS * RF
CHUNK = 256


class Place:
    def __init__(self):
        dp, ex = lax.axis_index("dp"), lax.axis_index("expert")
        self.dp, self.ex = dp, ex
        self.x, self.y = lax.rem(dp, NX), lax.div(dp, NX)
        self.z, self.c = lax.div(ex, 2), lax.rem(ex, 2)

    def xy(self, dx, dy):
        return lax.rem(self.y + dy + NX, NX) * NX + lax.rem(self.x + dx + NX, NX)

    def zz(self, dz):
        return lax.rem(self.z + dz + NZ, NZ)

    def dev_xy(self, dx, dy):
        return (self.xy(dx, dy), self.ex)

    def dev_z(self, dz):
        return (self.dp, self.zz(dz) * 2 + self.c)

    def partner(self):
        return (self.dp, self.z * 2 + 1 - self.c)


def barrier(devices):
    sem = pltpu.get_barrier_semaphore()
    for d in devices:
        pl.semaphore_signal(sem, inc=1, device_id=d, device_id_type=MESH)
    pl.semaphore_wait(sem, len(devices))


class Sender:
    def __init__(self, send_sem, recv_sem):
        self.send_sem, self.recv_sem = send_sem, recv_sem
        self.count = 0
        self.sent = []

    def send(self, src, dst, device):
        n = self.count
        self.count += 1
        cp = pltpu.make_async_remote_copy(
            src_ref=src, dst_ref=dst, send_sem=self.send_sem.at[n], recv_sem=self.recv_sem.at[n],
            device_id=device, device_id_type=MESH,
        )
        cp.start()
        self.sent.append(cp)
        return n

    def arrived(self, n, region, device):
        pltpu.make_async_remote_copy(
            src_ref=region, dst_ref=region, send_sem=self.send_sem.at[n], recv_sem=self.recv_sem.at[n],
            device_id=device, device_id_type=MESH,
        ).wait_recv()

    def finish(self):
        for cp in self.sent:
            cp.wait_send()


def gather_z(me, tx, own, region):
    c = me.c
    half = own.shape[0] // 2

    def part(ref, h):
        return ref if h is None else ref.at[pl.ds(h * half, half)]

    plus = tx.send(own, region(me.z, c, None), me.dev_z(1))
    minus = tx.send(own, region(me.z, c, None), me.dev_z(-1))
    got = [(tx.send(own, region(me.z, c, None), me.partner()), 0, None)]
    yield
    for k in (1, 2, 3):
        zl, zr = me.zz(-k), me.zz(k)
        tx.arrived(plus, region(zl, c, None), me.dev_z(1))
        plus = (tx.send(region(zl, c, None), region(zl, c, None), me.dev_z(1)) if k < 3
                else tx.send(region(zl, c, 0), region(zl, c, 0), me.dev_z(1)))
        got.append((tx.send(region(zl, c, None), region(zl, c, None), me.partner()), -k, None))
        tx.arrived(minus, region(zr, c, None), me.dev_z(-1))
        minus = (tx.send(region(zr, c, None), region(zr, c, None), me.dev_z(-1)) if k < 3
                 else tx.send(region(zr, c, 1), region(zr, c, 1), me.dev_z(-1)))
        got.append((tx.send(region(zr, c, None), region(zr, c, None), me.partner()), k, None))
        yield
    zo = me.zz(4)
    tx.arrived(plus, region(zo, c, 0), me.dev_z(1))
    got.append((tx.send(region(zo, c, 0), region(zo, c, 0), me.partner()), 4, 0))
    tx.arrived(minus, region(zo, c, 1), me.dev_z(-1))
    got.append((tx.send(region(zo, c, 1), region(zo, c, 1), me.partner()), 4, 1))
    yield
    for n, k, h in got:
        tx.arrived(n, region(me.zz(k), 1 - c, h), me.partner())
    yield


def gather_xy(me, tx, own, region, x_first):
    def idx(p, q):
        return me.xy(p, q) if x_first else me.xy(q, p)

    def dev(p, q):
        return me.dev_xy(p, q) if x_first else me.dev_xy(q, p)

    def src(p, q, h):
        return own(h) if (p, q) == (0, 0) else region(idx(p, q), h)

    def ring(p, q, dp_, dq_):
        return (tx.send(src(p, q, None), region(idx(p, q), None), dev(dp_, dq_)),
                tx.send(src(p, q, None), region(idx(p, q), None), dev(-dp_, -dq_)))

    def relay(n, p, q, dp_, dq_, h):
        tx.arrived(n, region(idx(p, q), None), dev(dp_, dq_))
        return tx.send(region(idx(p, q), h), region(idx(p, q), h), dev(dp_, dq_))

    far = {}

    def along_q(p):
        a, b = second[p]
        far[p] = (relay(a, p, -1, 0, 1, 0), relay(b, p, 1, 0, -1, 1))

    def opposite(p):
        for h in (0, 1):
            tx.arrived(far[p][h], region(idx(p, 2), h), dev(0, 1))

    first = ring(0, 0, 1, 0)
    second = {0: ring(0, 0, 0, 1)}
    yield
    o0 = relay(first[0], -1, 0, 1, 0, 0)
    second[-1] = ring(-1, 0, 0, 1)
    o1 = relay(first[1], 1, 0, -1, 0, 1)
    second[1] = ring(1, 0, 0, 1)
    along_q(0)
    yield
    tx.arrived(o0, region(idx(2, 0), 0), dev(1, 0))
    tx.arrived(o1, region(idx(2, 0), 1), dev(-1, 0))
    second[2] = ring(2, 0, 0, 1)
    along_q(-1)
    along_q(1)
    if not x_first:
        opposite(0)
    yield
    along_q(2)
    if not x_first:
        opposite(-1)
        opposite(1)
    yield
    for p in (0, -1, 1, 2) if x_first else (2,):
        opposite(p)
    yield


def split2(v):
    hi = v.astype(BF)
    return hi, (v - hi.astype(F32)).astype(BF)


def dot(a, b):
    return jnp.dot(a, b, preferred_element_type=F32)


def tables(meta):
    ex = lax.axis_index("expert").astype(F32)
    row = lax.broadcasted_iota(jnp.int32, (BLOCK, BLOCK), 0)
    col = lax.broadcasted_iota(jnp.int32, (BLOCK, BLOCK), 1)
    before = (row < col).astype(BF)
    quarter = lax.rem(lax.broadcasted_iota(jnp.int32, (GROUP, BLOCK), 0), 4).astype(F32)

    def one(ids, shares, which, cap):
        hit = (ids == which).astype(F32)
        named = jnp.sum(hit, axis=1)
        share = jnp.sum(hit * shares, axis=1)
        pos = dot(named.astype(BF), before) + quarter * cap
        return jnp.where(named > 0, pos, -1.0), share

    fid, pid, fsh, psh = (meta[:, 4 * i:4 * i + 4, :] for i in range(4))
    a = one(fid, fsh, 2.0 * ex, CAPF)
    b = one(fid, fsh, 2.0 * ex + 1.0, CAPF)
    p = one(pid, psh, ex, CAPP)
    return a, b, p


def quad_row(v, q):
    return jnp.concatenate([v[4 * q + i:4 * q + i + 1, :] for i in range(4)], axis=1)


def quad_col(v, first, q):
    return jnp.concatenate([v[:, first + 4 * q + i:first + 4 * q + i + 1] for i in range(4)], axis=0)


def pick(rows, pos):
    slot = lax.broadcasted_iota(jnp.int32, (rows, TOKQ), 0).astype(F32)
    return (slot == pos).astype(BF)


def put(rows, pos, share):
    slot = lax.broadcasted_iota(jnp.int32, (TOKQ, rows), 1).astype(F32)
    return jnp.where(slot == pos, share, 0.0)


STRIPES = 4
COLS = WIDTH // STRIPES
ORDER = (4, 3, -3, 2, -2, 1, -1, 0)
SENDS = 6 * 20 + 2 * 17 + STRIPES * (8 + 14 + 17)


def reduce_stripe(me, tx, ci, cols, part, theirs, ring, own, out, loc_sem):
    half = BLOCK // 2

    def mine(k, h=None):
        at = slice(None) if h is None else pl.ds(h * half, half)
        return part.at[me.zz(k) * 2 + me.c, at, cols]

    swap = {k: tx.send(part.at[me.zz(k) * 2 + 1 - me.c, :, cols], theirs.at[ci, me.zz(k)], me.partner()) for k in ORDER}
    yield

    def pair_sum(k):
        tx.arrived(swap[k], theirs.at[ci, me.zz(k)], me.partner())
        r = mine(k)
        r[...] = (r[...].astype(F32) + theirs[ci, me.zz(k)].astype(F32)).astype(BF)

    slot, waiting = {}, {}

    def push(sign, h, j):
        r = mine(sign * j, h)
        if (sign, h) in waiting:
            n, s = waiting[(sign, h)]
            tx.arrived(n, ring.at[ci, s], me.dev_z(sign))
            r[...] = (r[...].astype(F32) + ring[ci, s].astype(F32)).astype(BF)
        s = slot.setdefault((sign, h, j), len(slot))
        waiting[(sign, h)] = (tx.send(r, ring.at[ci, s], me.dev_z(sign)), s)

    pair_sum(4)
    push(1, 0, 4)
    push(-1, 1, 4)
    pair_sum(3)
    pair_sum(-3)
    push(1, 1, 3)
    push(-1, 0, 3)
    yield
    for j in (3, 2, 1):
        if j < 3:
            pair_sum(j)
            pair_sum(-j)
            push(1, 1, j)
            push(-1, 0, j)
        push(1, 0, j)
        push(-1, 1, j)
        yield
    pair_sum(0)
    for h in (1, 0):
        total = mine(0, h)[...].astype(F32)
        for sign in (1, -1):
            n, s = waiting[(sign, h)]
            tx.arrived(n, ring.at[ci, s], me.dev_z(sign))
            total = total + ring[ci, s].astype(F32)
        own[ci, pl.ds(h * half, half)] = total.astype(BF)

    def region(z, c, h):
        at = slice(None) if h is None else pl.ds(h * half, half)
        return out.at[z * 2 + c, at, cols]

    last = pltpu.make_async_copy(own.at[ci], out.at[me.ex, :, cols], loc_sem)
    last.start()
    yield from gather_z(me, tx, own.at[ci], region)
    last.wait()
    yield


def main_kernel(gate_i, up_i, down_i, tok_i, meta_i, first, second, res_o, meta_o, hid_o, low_o,
                gate, up, down, tok, meta, x0, x1, acc, h0, h1, wt, low3, b3, rows, theirs, ring, own,
                send_sem, recv_sem, loc_sem):
    me = Place()
    tx = Sender(send_sem, recv_sem)
    mine = pl.ds(pl.multiple_of(me.dp * BLOCK, BLOCK), BLOCK)
    loads = [
        pltpu.make_async_copy(s, d, loc_sem.at[i]) for i, (s, d) in enumerate((
            (meta_i, meta.at[me.ex]), (tok_i, tok.at[me.ex]), (gate_i, gate.at[:, mine, :]),
            (up_i, up.at[:, mine, :]), (down_i, down.at[:, :, mine])))
    ]
    for cp in loads:
        cp.start()
    barrier([me.dev_xy(1, 0), me.dev_xy(-1, 0), me.dev_xy(0, 1), me.dev_xy(0, -1),
             me.dev_z(1), me.dev_z(-1), me.partner()])

    def block_region(ref, size):
        def region(z, c, h):
            v = ref.at[z * 2 + c]
            return v if h is None else v.at[pl.ds(h * (size // 2), size // 2)]
        return region

    def rows_region(ref, e):
        def region(dp, h):
            if h is None:
                return ref.at[e, pl.ds(pl.multiple_of(dp * BLOCK, BLOCK), BLOCK), :]
            n = BLOCK // 2
            return ref.at[e, pl.ds(pl.multiple_of(dp * BLOCK + h * n, n), n), :]
        return region

    def cols_region(ref, e):
        def region(dp, h):
            cols = pl.ds(pl.multiple_of(dp * BLOCK, BLOCK), BLOCK)
            if h is None:
                return ref.at[e, :, cols]
            return ref.at[e, pl.ds(h * (HIDDEN // 2), HIDDEN // 2), cols]
        return region

    def own_half(ref, e):
        def half(h):
            v = ref.at[e]
            n = v.shape[0] // 2
            return v if h is None else v.at[pl.ds(h * n, n)]
        return half

    def jobs(ref, region_of, out):
        return [gather_xy(me, tx, own_half(ref, e), region_of(out, e), e == 0) for e in (0, 1)]

    meta_j = gather_z(me, tx, meta_i, block_region(meta, 16))
    tok_j = gather_z(me, tx, tok_i, block_region(tok, BLOCK))
    gate_j = jobs(gate_i, rows_region, gate)
    up_j = jobs(up_i, rows_region, up)
    down_j = jobs(down_i, cols_region, down)

    def step(*js):
        for j in js:
            next(j, None)

    step(meta_j)
    step(*gate_j)
    step(tok_j)
    step(*up_j)
    bh, bl = split2(second[0])
    b3[0:RANK], b3[RANK:2 * RANK], b3[2 * RANK:] = bh, bh, bl
    step(*gate_j)
    step(meta_j, tok_j)
    step(*up_j)
    step(*gate_j)
    step(meta_j, tok_j)
    step(*up_j)
    step(meta_j, tok_j)
    step(*gate_j)
    step(meta_j, tok_j)
    tok_last = tx.count
    step(meta_j, tok_j)
    step(*up_j)
    step(*down_j)
    for cp in loads:
        cp.wait()

    tab = tables(meta[...])
    (pa, wa), (pb, wb), (pp, wp) = tab
    turned = jnp.transpose(jnp.concatenate([pa, pb, pp, -wa, -wb, wp, pp, wp], axis=0))
    for q in range(QUADS):
        wt[q] = jnp.concatenate([
            put(RF, quad_col(turned, 0, q), quad_col(turned, 48, q)),
            put(RP, quad_col(turned, 32, q), quad_col(turned, 80, q)),
            put(RF, quad_col(turned, 16, q), quad_col(turned, 64, q)),
        ], axis=1).astype(BF)

    for q in range(QUADS):
        oa, op, ob = pick(RF, quad_row(pa, q)), pick(RP, quad_row(pp, q)), pick(RF, quad_row(pb, q))

        def gather(i, _):
            at = pl.ds(pl.multiple_of(i * 512, 512), 512)
            t = tok[4 * q:4 * q + 4, :, at].reshape(TOKQ, 512)
            x0[q * RF:(q + 1) * RF, at] = dot(oa, t).astype(BF)
            x0[QUADS * RF + q * RP:QUADS * RF + (q + 1) * RP, at] = dot(op, t).astype(BF)
            x1[q * RF:(q + 1) * RF, at] = dot(ob, t).astype(BF)
            return 0

        lax.fori_loop(0, 4, gather, 0)

    def stripe(r):
        return pl.ds(pl.multiple_of(lax.rem(me.y + r + NX, NX) * COLS, COLS), COLS)

    def early(x, e, m, first_row):
        rows_m = x.shape[0] // m

        def body(i, _):
            lo = pl.multiple_of(lax.rem(i, m) * rows_m, rows_m)
            rr = pl.ds(lo, rows_m)
            ra = pl.ds(first_row + lo, rows_m)
            cc = pl.ds(pl.multiple_of(lax.div(i, m) * CHUNK, CHUNK), CHUNK)
            for w, ref in enumerate((gate, up)):
                acc[w, ra, cc] = sum(dot(x[rr, stripe(r)], ref[e, stripe(r), cc]) for r in (0, -1, 1))
            return 0

        lax.fori_loop(0, m * (HIDDEN // CHUNK), body, 0)

    def late(x, h, e, m, first_row):
        rows_m = x.shape[0] // m

        def body(i, _):
            lo = pl.multiple_of(lax.rem(i, m) * rows_m, rows_m)
            rr = pl.ds(lo, rows_m)
            ra = pl.ds(first_row + lo, rows_m)
            cc = pl.ds(pl.multiple_of(lax.div(i, m) * CHUNK, CHUNK), CHUNK)
            g = acc[0, ra, cc] + dot(x[rr, stripe(2)], gate[e, stripe(2), cc])
            u = acc[1, ra, cc] + dot(x[rr, stripe(2)], up[e, stripe(2), cc])
            h[rr, cc] = (g / (1.0 + jnp.exp(-g)) * u).astype(BF)
            return 0

        lax.fori_loop(0, m * (HIDDEN // CHUNK), body, 0)

    early(x0, 0, 2, 0)
    early(x1, 1, 1, ROWS0)
    step(*gate_j)
    step(*up_j)
    step(*down_j)
    late(x0, h0, 0, 2, 0)
    late(x1, h1, 1, 1, ROWS0)
    step(*down_j)

    hid = h0[QUADS * RF:, :]
    ah, al = split2(first[0])
    low2 = dot(hid, jnp.concatenate([ah, al], axis=1))
    low = low2[:, :RANK] + low2[:, RANK:]
    lh, ll = split2(low)
    low3[...] = jnp.concatenate([lh, ll, lh], axis=1)
    hid_o[...] = hid
    low_o[...] = low
    meta_o[...] = meta[...]
    for cp in tx.sent[:tok_last]:
        cp.wait_send()
    del tx.sent[:tok_last]

    def partial(r):
        base = lax.rem(me.y + r + NX, NX) * COLS

        def body(i, _):
            at = pl.ds(pl.multiple_of(base + i * CHUNK, CHUNK), CHUNK)
            r0 = dot(h0[...], down[0, :, at])
            rp = r0[QUADS * RF:] + dot(low3[...], b3[:, at])
            r1 = dot(h1[...], down[1, :, at])
            for q in range(QUADS):
                rows[q, 0:RF] = r0[q * RF:(q + 1) * RF].astype(BF)
                rows[q, RF:RF + RP] = rp[q * RP:(q + 1) * RP].astype(BF)
                rows[q, RF + RP:] = r1[q * RF:(q + 1) * RF].astype(BF)
            for q in range(QUADS):
                tok[4 * q:4 * q + 4, :, at] = dot(wt[q], rows[q]).astype(BF).reshape(4, BLOCK, CHUNK)
            return 0

        lax.fori_loop(0, COLS // CHUNK, body, 0)

    red = [reduce_stripe(me, tx, i, stripe(r), tok, theirs, ring, own, res_o, loc_sem.at[5 + i])
           for i, r in enumerate((0, -1, 1, 2))]
    partial(0)
    step(red[0])
    step(*down_j)
    partial(-1)
    step(red[1], red[0])
    partial(1)
    step(red[0], red[2], red[1])
    step(*down_j)
    partial(2)
    step(red[3])
    for _ in range(14):
        step(*red)
    assert tx.count == SENDS
    tx.finish()


def main_call(gate, up, down, tok, meta, first, second):
    sds = jax.ShapeDtypeStruct
    vm = pltpu.VMEM
    return pl.pallas_call(
        main_kernel,
        out_shape=(sds((GROUP, BLOCK, WIDTH), BF), sds((GROUP, 16, BLOCK), F32),
                   sds((QUADS * RP, HIDDEN), BF), sds((QUADS * RP, RANK), F32)),
        in_specs=[ANY] * 5 + [VM] * 2,
        out_specs=(ANY, VM, VM, VM),
        scratch_shapes=[
            vm((2, WIDTH, HIDDEN), BF), vm((2, WIDTH, HIDDEN), BF), vm((2, HIDDEN, WIDTH), BF),
            vm((GROUP, BLOCK, WIDTH), BF), vm((GROUP, 16, BLOCK), F32),
            vm((ROWS0, WIDTH), BF), vm((ROWS1, WIDTH), BF), vm((2, ROWS0 + ROWS1, HIDDEN), F32),
            vm((ROWS0, HIDDEN), BF), vm((ROWS1, HIDDEN), BF),
            vm((QUADS, TOKQ, RQ), BF), vm((QUADS * RP, 3 * RANK), BF), vm((3 * RANK, WIDTH), BF),
            vm((QUADS, RQ, CHUNK), BF),
            vm((STRIPES, NZ, BLOCK, COLS), BF), vm((STRIPES, 14, BLOCK // 2, COLS), BF), vm((STRIPES, BLOCK, COLS), BF),
            pltpu.SemaphoreType.DMA((SENDS,)), pltpu.SemaphoreType.DMA((SENDS,)), pltpu.SemaphoreType.DMA((9,)),
        ],
        compiler_params=pltpu.CompilerParams(collective_id=0, has_side_effects=True, vmem_limit_bytes=62 << 20),
        name="main",
    )(gate, up, down, tok, meta, first, second)


def grads_kernel(res_h, meta, hid, low, second, ga_o, gb_o, res, back, sems):
    loads = []
    for q in range(QUADS):
        loads.append(pltpu.make_async_copy(res_h.at[pl.ds(4 * q, 4)], res.at[pl.ds(4 * q, 4)], sems.at[q]))
    for cp in loads:
        cp.start()
    (_, _), (_, _), (pp, wp) = tables(meta[...])
    bh, bl = split2(second[0])
    b2 = jnp.concatenate([bh, bl], axis=0)
    nt = (((1,), (1,)), ((), ()))
    tn = (((0,), (0,)), ((), ()))
    gb = jnp.zeros((2 * RANK, WIDTH), F32)
    for q in range(QUADS):
        op = pick(RP, quad_row(pp, q))
        share = quad_row(wp, q)
        lq = low[q * RP:(q + 1) * RP, :]
        l1 = lq.astype(BF)
        r1 = lq - l1.astype(F32)
        l2 = r1.astype(BF)
        l3 = (r1 - l2.astype(F32)).astype(BF)
        spread = lax.dot_general(jnp.concatenate([l1, l2, l3, jnp.zeros_like(l1)], axis=1), op, tn,
                                 preferred_element_type=F32)
        low_t = (spread[0:RANK] + spread[RANK:2 * RANK] + spread[2 * RANK:3 * RANK]) * share
        th, tl = split2(low_t)
        loads[q].wait()
        rq = res[4 * q:4 * q + 4].reshape(TOKQ, WIDTH)
        gb = gb + dot(jnp.concatenate([th, tl], axis=0), rq)
        bt = lax.dot_general(b2, rq, nt, preferred_element_type=F32)
        bt = (bt[:RANK] + bt[RANK:]) * share
        b_hi, b_lo = split2(bt)
        picked = lax.dot_general(op, jnp.concatenate([b_hi, b_lo], axis=0), nt, preferred_element_type=F32)
        back[q * RP:(q + 1) * RP, :] = picked.astype(BF)
    gb_o[...] = gb[:RANK] + gb[RANK:]
    ga = lax.dot_general(hid[...], back[...], tn, preferred_element_type=F32)
    ga_o[...] = ga[:, :RANK] + ga[:, RANK:]


def grads(res, meta, hid, low, second):
    sds = jax.ShapeDtypeStruct
    vm = pltpu.VMEM
    return pl.pallas_call(
        grads_kernel,
        out_shape=(sds((HIDDEN, RANK), F32), sds((RANK, WIDTH), F32)),
        in_specs=[ANY] + [VM] * 4,
        out_specs=(VM, VM),
        scratch_shapes=[vm((GROUP, BLOCK, WIDTH), BF), vm((QUADS * RP, 2 * RANK), BF), pltpu.SemaphoreType.DMA((QUADS,))],
        compiler_params=pltpu.CompilerParams(vmem_limit_bytes=60 << 20),
        name="grads",
    )(res, meta, hid, low, second)


def exchange_kernel(pa, pb, ga, gb, ra, rb, send_sem, recv_sem):
    dp, ex = lax.axis_index("dp"), lax.axis_index("expert")
    tx = Sender(send_sem, recv_sem)
    na, nb = HIDDEN // GROUP, WIDTH // GROUP

    def dev(o):
        return (lax.rem(dp + o, GROUP), ex)

    barrier([dev(o) for o in range(1, GROUP)])
    got = []
    for o in range(1, GROUP):
        d = lax.rem(dp + o, GROUP)
        got.append(tx.send(pa.at[pl.ds(pl.multiple_of(d * na, na), na)], ra.at[o - 1], dev(o)))
        got.append(tx.send(pb.at[:, pl.ds(pl.multiple_of(d * nb, nb), nb)], rb.at[o - 1], dev(o)))
    ta = pa[pl.ds(pl.multiple_of(dp * na, na), na), :]
    tb = pb[:, pl.ds(pl.multiple_of(dp * nb, nb), nb)]
    for o in range(1, GROUP):
        tx.arrived(got[2 * o - 2], ra.at[o - 1], dev(o))
        tx.arrived(got[2 * o - 1], rb.at[o - 1], dev(o))
        ta = ta + ra[o - 1]
        tb = tb + rb[o - 1]
    ga[...] = ta
    gb[...] = tb
    tx.finish()


def exchange(pa, pb):
    sds = jax.ShapeDtypeStruct
    vm = pltpu.VMEM
    na, nb = HIDDEN // GROUP, WIDTH // GROUP
    n = 2 * (GROUP - 1)
    return pl.pallas_call(
        exchange_kernel,
        out_shape=(sds((na, RANK), F32), sds((RANK, nb), F32)),
        in_specs=[VM, VM],
        out_specs=(VM, VM),
        scratch_shapes=[
            vm((GROUP - 1, na, RANK), F32), vm((GROUP - 1, RANK, nb), F32),
            pltpu.SemaphoreType.DMA((n,)), pltpu.SemaphoreType.DMA((n,)),
        ],
        compiler_params=pltpu.CompilerParams(collective_id=2, has_side_effects=True),
        name="exchange",
    )(pa, pb)


def shards(tokens, fid, pid, fsc, psc, gate, up, down, first, second):
    fsh = fsc / jnp.sum(fsc, axis=1, keepdims=True)
    psh = psc / jnp.sum(psc, axis=1, keepdims=True)
    meta = jnp.concatenate([fid.astype(F32), pid.astype(F32), fsh, psh], axis=1).T
    res, meta_f, hid, low = main_call(gate, up, down, tokens, meta, first, second)
    pa, pb = grads(res, meta_f, hid, low, second)
    ga, gb = exchange(pa, pb)
    return ga[None], gb[None]


def solution(mesh):
    rows = P(("dp", "expert"), None)
    return jax.shard_map(
        shards,
        mesh=mesh,
        in_specs=(rows,) * 5 + (P("expert", "dp", None), P("expert", "dp", None), P("expert", None, "dp"),
                                P("expert", None, None), P("expert", None, None)),
        out_specs=(P("expert", "dp", None), P("expert", None, "dp")),
        check_vma=False,
    )
```

time: 280 us -> 245 us (0.88)
  Pallas kernels: 270 us -> 236 us
    pallas_call x3 -> x1, Pallas kernels: 242 us -> 208 us  [main_call(): pl.pallas_call(main_kernel, out_shape=(sds((GROUP, BLOCK, WIDTH), BF), sd...]
where the time goes in v2:
time: 245 us
  Pallas kernels  236 us (96%)
  local copies, waits for them, and re-layouts  4.6 us (2%)
  other arithmetic  4.08 us (2%)
    pallas_call x1, Pallas kernels, main_call(): pl.pallas_call(main_kernel, out_shape=(sds((GROUP, BLOCK, WIDTH), BF), sd...  208 us
    pallas_call x1, Pallas kernels, exchange(): pl.pallas_call(exchange_kernel, out_shape=(sds((na, RANK), F32), sds((RAN...  18.3 us
    pallas_call x1, Pallas kernels, grads(): pl.pallas_call(grads_kernel, out_shape=(sds((HIDDEN, RANK), F32), sds((RA...  9.72 us

profile of v2, /device:TPU:1, one launch (start us, length us, event | category | flops | bytes accessed | tf_op | source)
XLA Modules:
  0.0 245.0 jit_solution(9118737608716830783)
XLA Ops:
  0.6 0.7 reduce_sum.18
  1.3 0.7 reduce_sum.19
  2.0 0.7 convert_element_type.6
  2.7 0.7 convert_element_type.7
  3.4 0.7 broadcast_divide_fusion
  4.1 0.6 maximum_bitcast_fusion.meta_i
  4.7 1.9 copy.12.first
  6.6 207.6 %main.1 = (bf16[16,128,2048]{2,1,0:T(8,128)(2,1)}, f32[16,16,128]{2,1,0:T(8,128)}, bf16[576,768]{1,0:T(8,128)(2,1)}, f32[576,64]{1,0:T(8,128)}) custom-call(bf16[2,128,768]{2,1,0:T(8,128)(2,1)} %gate_i.1, bf16[2,128,768]{2,1,0:T(8,128)(2,1)} %up_i.1, bf16[2,768,128]{2,1,0:T(8,128)(2,1)} %down_i.1, bf16[128,2048]{1,0:T(8,128)(2,1)} %tok_i.1, ...), custom_call_target="tpu_custom_call" | custom-call | tf_op jit(solution)/shard_map/main/pallas_call | solution.py:494
  214.2 9.7 %grads.1 = (f32[768,64]{1,0:T(8,128)}, f32[64,2048]{1,0:T(8,128)}) custom-call(bf16[16,128,2048]{2,1,0:T(8,128)(2,1)} %get-tuple-element.10.res_h, f32[16,16,128]{2,1,0:T(8,128)} %get-tuple-element.11.meta, bf16[576,768]{1,0:T(8,128)(2,1)} %get-tuple-element.12.hid, f32[576,64]{1,0:T(8,128)} %get-tuple-element.13.low, f32[1,64,2048]{2,1,0:T(8,128)} %second.3), custom_call_target="tpu_custom_call" | custom-call | tf_op jit(solution)/shard_map/grads/pallas_call | solution.py:555
  223.9 18.3 %exchange.1 = (f32[48,64]{1,0:T(8,128)}, f32[64,128]{1,0:T(8,128)}) custom-call(f32[768,64]{1,0:T(8,128)} %get-tuple-element.14.pa, f32[64,2048]{1,0:T(8,128)} %get-tuple-element.15.pb), custom_call_target="tpu_custom_call" | custom-call | tf_op jit(solution)/shard_map/exchange/pallas_call | solution.py:597
  242.2 1.3 copy.15
  243.6 1.4 copy.16

commit v3 on v2

v3 whole, which is shorter than its diff:
```python
import functools

import jax
import jax.numpy as jnp
from jax import lax
from jax.experimental import pallas as pl
from jax.experimental.pallas import tpu as pltpu
from jax.sharding import PartitionSpec as P

BF = jnp.bfloat16
F32 = jnp.float32
MESH = pl.DeviceIdType.MESH
ANY = pl.BlockSpec(memory_space=pl.ANY)
VM = pl.BlockSpec(memory_space=pltpu.VMEM)

NX = 4
NZ = 8
GROUP = 16
BLOCK = 128
WIDTH = 2048
HIDDEN = 768
RANK = 64
QUADS = 4
TOKQ = 4 * BLOCK
CAPF = 18
CAPP = 36
RF = 80
RP = 144
RQ = 2 * RF + RP
ROWS0 = QUADS * (RF + RP)
ROWS1 = QUADS * RF
CHUNK = 256


class Place:
    def __init__(self):
        dp, ex = lax.axis_index("dp"), lax.axis_index("expert")
        self.dp, self.ex = dp, ex
        self.x, self.y = lax.rem(dp, NX), lax.div(dp, NX)
        self.z, self.c = lax.div(ex, 2), lax.rem(ex, 2)

    def xy(self, dx, dy):
        return lax.rem(self.y + dy + NX, NX) * NX + lax.rem(self.x + dx + NX, NX)

    def zz(self, dz):
        return lax.rem(self.z + dz + NZ, NZ)

    def dev_xy(self, dx, dy):
        return (self.xy(dx, dy), self.ex)

    def dev_z(self, dz):
        return (self.dp, self.zz(dz) * 2 + self.c)

    def partner(self):
        return (self.dp, self.z * 2 + 1 - self.c)


def barrier(devices):
    sem = pltpu.get_barrier_semaphore()
    for d in devices:
        pl.semaphore_signal(sem, inc=1, device_id=d, device_id_type=MESH)
    pl.semaphore_wait(sem, len(devices))


class Sender:
    def __init__(self, send_sem, recv_sem):
        self.send_sem, self.recv_sem = send_sem, recv_sem
        self.count = 0
        self.sent = []
        self.tag = None

    def send(self, src, dst, device):
        n = self.count
        self.count += 1
        cp = pltpu.make_async_remote_copy(
            src_ref=src, dst_ref=dst, send_sem=self.send_sem.at[n], recv_sem=self.recv_sem.at[n],
            device_id=device, device_id_type=MESH,
        )
        cp.start()
        self.sent.append((self.tag, cp))
        return n

    def arrived(self, n, region, device):
        pltpu.make_async_remote_copy(
            src_ref=region, dst_ref=region, send_sem=self.send_sem.at[n], recv_sem=self.recv_sem.at[n],
            device_id=device, device_id_type=MESH,
        ).wait_recv()

    def drain(self, tags):
        for tag, cp in self.sent:
            if tag in tags:
                cp.wait_send()
        self.sent = [(tag, cp) for tag, cp in self.sent if tag not in tags]


def gather_z(me, tx, own, region):
    c = me.c
    plus = tx.send(own, region(me.z, c, None), me.dev_z(1))
    minus = tx.send(own, region(me.z, c, None), me.dev_z(-1))
    got = [(tx.send(own, region(me.z, c, None), me.partner()), 0, None)]
    yield
    for k in (1, 2, 3):
        zl, zr = me.zz(-k), me.zz(k)
        tx.arrived(plus, region(zl, c, None), me.dev_z(1))
        plus = (tx.send(region(zl, c, None), region(zl, c, None), me.dev_z(1)) if k < 3
                else tx.send(region(zl, c, 0), region(zl, c, 0), me.dev_z(1)))
        got.append((tx.send(region(zl, c, None), region(zl, c, None), me.partner()), -k, None))
        tx.arrived(minus, region(zr, c, None), me.dev_z(-1))
        minus = (tx.send(region(zr, c, None), region(zr, c, None), me.dev_z(-1)) if k < 3
                 else tx.send(region(zr, c, 1), region(zr, c, 1), me.dev_z(-1)))
        got.append((tx.send(region(zr, c, None), region(zr, c, None), me.partner()), k, None))
        yield
    zo = me.zz(4)
    tx.arrived(plus, region(zo, c, 0), me.dev_z(1))
    got.append((tx.send(region(zo, c, 0), region(zo, c, 0), me.partner()), 4, 0))
    tx.arrived(minus, region(zo, c, 1), me.dev_z(-1))
    got.append((tx.send(region(zo, c, 1), region(zo, c, 1), me.partner()), 4, 1))
    yield
    for n, k, h in got:
        tx.arrived(n, region(me.zz(k), 1 - c, h), me.partner())
    yield


def gather_xy(me, tx, own, region, x_first):
    def idx(p, q):
        return me.xy(p, q) if x_first else me.xy(q, p)

    def dev(p, q):
        return me.dev_xy(p, q) if x_first else me.dev_xy(q, p)

    def src(p, q, h):
        return own(h) if (p, q) == (0, 0) else region(idx(p, q), h)

    def ring(p, q, dp_, dq_):
        return (tx.send(src(p, q, None), region(idx(p, q), None), dev(dp_, dq_)),
                tx.send(src(p, q, None), region(idx(p, q), None), dev(-dp_, -dq_)))

    def relay(n, p, q, dp_, dq_, h):
        tx.arrived(n, region(idx(p, q), None), dev(dp_, dq_))
        return tx.send(region(idx(p, q), h), region(idx(p, q), h), dev(dp_, dq_))

    far = {}

    def along_q(p):
        a, b = second[p]
        far[p] = (relay(a, p, -1, 0, 1, 0), relay(b, p, 1, 0, -1, 1))

    def opposite(p):
        for h in (0, 1):
            tx.arrived(far[p][h], region(idx(p, 2), h), dev(0, 1))

    first = ring(0, 0, 1, 0)
    second = {0: ring(0, 0, 0, 1)}
    yield
    o0 = relay(first[0], -1, 0, 1, 0, 0)
    o1 = relay(first[1], 1, 0, -1, 0, 1)
    second[-1] = ring(-1, 0, 0, 1)
    second[1] = ring(1, 0, 0, 1)
    yield
    along_q(0)
    yield
    tx.arrived(o0, region(idx(2, 0), 0), dev(1, 0))
    tx.arrived(o1, region(idx(2, 0), 1), dev(-1, 0))
    second[2] = ring(2, 0, 0, 1)
    yield
    if not x_first:
        opposite(0)
    yield
    along_q(-1)
    along_q(1)
    yield
    along_q(2)
    yield
    if not x_first:
        opposite(-1)
        opposite(1)
    yield
    for p in (0, -1, 1, 2) if x_first else (2,):
        opposite(p)
    yield


def split2(v):
    hi = v.astype(BF)
    return hi, (v - hi.astype(F32)).astype(BF)


def dot(a, b):
    return jnp.dot(a, b, preferred_element_type=F32)


def tables(meta):
    ex = lax.axis_index("expert").astype(F32)
    row = lax.broadcasted_iota(jnp.int32, (BLOCK, BLOCK), 0)
    col = lax.broadcasted_iota(jnp.int32, (BLOCK, BLOCK), 1)
    before = (row < col).astype(BF)
    quarter = lax.rem(lax.broadcasted_iota(jnp.int32, (GROUP, BLOCK), 0), 4).astype(F32)

    def one(ids, shares, which, cap):
        hit = (ids == which).astype(F32)
        named = jnp.sum(hit, axis=1)
        share = jnp.sum(hit * shares, axis=1)
        pos = dot(named.astype(BF), before) + quarter * cap
        return jnp.where(named > 0, pos, -1.0), share

    fid, pid, fsh, psh = (meta[:, 4 * i:4 * i + 4, :] for i in range(4))
    a = one(fid, fsh, 2.0 * ex, CAPF)
    b = one(fid, fsh, 2.0 * ex + 1.0, CAPF)
    p = one(pid, psh, ex, CAPP)
    return a, b, p


def quad_row(v, q):
    return jnp.concatenate([v[4 * q + i:4 * q + i + 1, :] for i in range(4)], axis=1)


def quad_col(v, first, q):
    return jnp.concatenate([v[:, first + 4 * q + i:first + 4 * q + i + 1] for i in range(4)], axis=0)


def pick(rows, pos):
    slot = lax.broadcasted_iota(jnp.int32, (rows, TOKQ), 0).astype(F32)
    return (slot == pos).astype(BF)


def put(rows, pos, share):
    slot = lax.broadcasted_iota(jnp.int32, (TOKQ, rows), 1).astype(F32)
    return jnp.where(slot == pos, share, 0.0)


STRIPES = 4
COLS = WIDTH // STRIPES
ROW_OF = (0, -1, 1, 2)
ORDER = (4, 3, -3, 2, -2, 1, -1, 0)
SENDS = 6 * 20 + 2 * 17 + STRIPES * (8 + 14 + 17) + 2 * (GROUP - 1)

PLAN = (
    "gummttdgugmmtmtutgmTgutgguQQQQugEgududFuLlWdddPP00dd0P0P101d",
    "0P101P201P21P32013231023132V130231C232C3232C3C",
)


def reduce_stripe(me, tx, ci, cols, part, theirs, ring, out):
    half = BLOCK // 2

    def mine(k, h=None):
        at = slice(None) if h is None else pl.ds(h * half, half)
        return part.at[me.zz(k) * 2 + me.c, at, cols]

    def region(z, c, h):
        lo = (z * 2 + c) * BLOCK
        if h is None:
            return out.at[ci, pl.ds(pl.multiple_of(lo, BLOCK), BLOCK), 0:COLS]
        return out.at[ci, pl.ds(pl.multiple_of(lo + h * half, half), half), 0:COLS]

    swap = {k: tx.send(part.at[me.zz(k) * 2 + 1 - me.c, :, cols], theirs.at[ci, me.zz(k)], me.partner()) for k in ORDER}
    yield

    def pair_sum(k):
        tx.arrived(swap[k], theirs.at[ci, me.zz(k)], me.partner())
        r = mine(k)
        r[...] = (r[...].astype(F32) + theirs[ci, me.zz(k)].astype(F32)).astype(BF)

    slot, waiting = {}, {}

    def push(sign, h, j):
        r = mine(sign * j, h)
        if (sign, h) in waiting:
            n, s = waiting[(sign, h)]
            tx.arrived(n, ring.at[ci, s], me.dev_z(sign))
            r[...] = (r[...].astype(F32) + ring[ci, s].astype(F32)).astype(BF)
        s = slot.setdefault((sign, h, j), len(slot))
        waiting[(sign, h)] = (tx.send(r, ring.at[ci, s], me.dev_z(sign)), s)

    pair_sum(4)
    push(1, 0, 4)
    push(-1, 1, 4)
    pair_sum(3)
    pair_sum(-3)
    push(1, 1, 3)
    push(-1, 0, 3)
    yield
    for j in (3, 2, 1):
        if j < 3:
            pair_sum(j)
            pair_sum(-j)
            push(1, 1, j)
            push(-1, 0, j)
        push(1, 0, j)
        push(-1, 1, j)
        yield
    pair_sum(0)
    for h in (1, 0):
        total = mine(0, h)[...].astype(F32)
        for sign in (1, -1):
            n, s = waiting[(sign, h)]
            tx.arrived(n, ring.at[ci, s], me.dev_z(sign))
            total = total + ring[ci, s].astype(F32)
        region(me.z, me.c, h)[...] = total.astype(BF)
    yield from gather_z(me, tx, region(me.z, me.c, None), region)


def main_kernel(gate_i, up_i, down_i, tok_i, fid_i, pid_i, fsc_i, psc_i, first, second, ga_o, gb_o,
                big, down, tok, meta, x0, x1, acc, h0, h1, wt, low_s, low3, b3, rows, theirs, ring,
                sel, low_t, bt, hid_t, back, gbuf, gabuf, ra, rb, send_sem, recv_sem, loc_sem):
    me = Place()
    tx = Sender(send_sem, recv_sem)
    mine = pl.ds(pl.multiple_of(me.dp * BLOCK, BLOCK), BLOCK)
    loads = [
        pltpu.make_async_copy(s, d, loc_sem.at[i]) for i, (s, d) in enumerate((
            (tok_i, tok.at[me.ex]), (gate_i, big.at[0:2, mine, :]),
            (up_i, big.at[2:4, mine, :]), (down_i, down.at[:, :, mine])))
    ]
    for cp in loads:
        cp.start()
    peers = [(dx, dy) for dy in ROW_OF for dx in range(NX)]
    barrier([me.dev_xy(*p) for p in peers if p != (0, 0)] + [me.dev_z(1), me.dev_z(-1), me.partner()])

    def block_region(ref, size):
        def region(z, c, h):
            v = ref.at[z * 2 + c]
            return v if h is None else v.at[pl.ds(h * (size // 2), size // 2)]
        return region

    def rows_region(i):
        def region(dp, h):
            if h is None:
                return big.at[i, pl.ds(pl.multiple_of(dp * BLOCK, BLOCK), BLOCK), :]
            n = BLOCK // 2
            return big.at[i, pl.ds(pl.multiple_of(dp * BLOCK + h * n, n), n), :]
        return region

    def cols_region(e):
        def region(dp, h):
            cols = pl.ds(pl.multiple_of(dp * BLOCK, BLOCK), BLOCK)
            if h is None:
                return down.at[e, :, cols]
            return down.at[e, pl.ds(h * (HIDDEN // 2), HIDDEN // 2), cols]
        return region

    def own_half(ref, e):
        def half(h):
            v = ref.at[e]
            n = v.shape[0] // 2
            return v if h is None else v.at[pl.ds(h * n, n)]
        return half

    def stripe(r):
        return pl.ds(pl.multiple_of(lax.rem(me.y + r + NX, NX) * COLS, COLS), COLS)

    jobs = {
        "m": [gather_z(me, tx, meta.at[me.ex], block_region(meta, 16))],
        "t": [gather_z(me, tx, tok_i, block_region(tok, BLOCK))],
        "g": [gather_xy(me, tx, own_half(gate_i, e), rows_region(e), e == 0) for e in (0, 1)],
        "u": [gather_xy(me, tx, own_half(up_i, e), rows_region(2 + e), e == 0) for e in (0, 1)],
        "d": [gather_xy(me, tx, own_half(down_i, e), cols_region(e), e == 0) for e in (0, 1)],
    }
    for i, r in enumerate(ROW_OF):
        jobs[str(i)] = [reduce_stripe(me, tx, i, stripe(r), tok, theirs, ring, big)]

    fsc, psc = fsc_i[...], psc_i[...]
    meta[me.ex] = jnp.concatenate([
        fid_i[...].astype(F32), pid_i[...].astype(F32),
        fsc / jnp.sum(fsc, axis=0, keepdims=True), psc / jnp.sum(psc, axis=0, keepdims=True)], axis=0)
    kept = {}

    def table_step():
        for cp in loads:
            cp.wait()
        bh, bl = split2(second[0])
        b3[0:RANK], b3[RANK:2 * RANK], b3[2 * RANK:] = bh, bh, bl
        (pa, wa), (pb, wb), (pp, wp) = tables(meta[...])
        turned = jnp.transpose(jnp.concatenate([pa, pb, pp, -wa, -wb, wp, pp, wp], axis=0))
        for q in range(QUADS):
            wt[q] = jnp.concatenate([
                put(RF, quad_col(turned, 0, q), quad_col(turned, 48, q)),
                put(RP, quad_col(turned, 32, q), quad_col(turned, 80, q)),
                put(RF, quad_col(turned, 16, q), quad_col(turned, 64, q)),
            ], axis=1).astype(BF)
        kept["rows"] = (pa, pb, pp)
        kept["share"] = wp
        kept["quad"] = iter(range(QUADS))
        kept["half"] = iter([(r, i) for r in ROW_OF for i in range(COLS // CHUNK)])
        kept["grad"] = iter(range(STRIPES))

    def gather_step():
        q = next(kept["quad"])
        pa, pb, pp = kept["rows"]
        oa, op, ob = pick(RF, quad_row(pa, q)), pick(RP, quad_row(pp, q)), pick(RF, quad_row(pb, q))
        sel[q] = op

        def body(i, _):
            at = pl.ds(pl.multiple_of(i * 512, 512), 512)
            t = tok[4 * q:4 * q + 4, :, at].reshape(TOKQ, 512)
            x0[q * RF:(q + 1) * RF, at] = dot(oa, t).astype(BF)
            x0[QUADS * RF + q * RP:QUADS * RF + (q + 1) * RP, at] = dot(op, t).astype(BF)
            x1[q * RF:(q + 1) * RF, at] = dot(ob, t).astype(BF)
            return 0

        lax.fori_loop(0, 4, body, 0)

    def product(x, e, m, first_row, parts, how, h=None):
        rows_m = x.shape[0] // m

        def body(i, _):
            lo = pl.multiple_of(lax.rem(i, m) * rows_m, rows_m)
            rr = pl.ds(lo, rows_m)
            ra_ = pl.ds(first_row + lo, rows_m)
            cc = pl.ds(pl.multiple_of(lax.div(i, m) * CHUNK, CHUNK), CHUNK)
            out = []
            for w in (0, 1):
                v = sum(dot(x[rr, stripe(r)], big[2 * w + e, stripe(r), cc]) for r in parts)
                out.append(v if how == "set" else acc[w, ra_, cc] + v)
            if how == "end":
                g, u = out
                h[rr, cc] = (g / (1.0 + jnp.exp(-g)) * u).astype(BF)
            else:
                acc[0, ra_, cc], acc[1, ra_, cc] = out
            return 0

        lax.fori_loop(0, m * (HIDDEN // CHUNK), body, 0)

    def row0_step():
        product(x0, 0, 2, 0, (0,), "set")
        product(x1, 1, 1, ROWS0, (0,), "set")

    def rows1_step():
        product(x0, 0, 2, 0, (-1, 1), "add")
        product(x1, 1, 1, ROWS0, (-1, 1), "add")

    def last0_step():
        product(x0, 0, 2, 0, (2,), "end", h0)

    def last1_step():
        product(x1, 1, 1, ROWS0, (2,), "end", h1)

    nt = (((1,), (1,)), ((), ()))
    tn = (((0,), (0,)), ((), ()))

    def low_step():
        tx.drain("mtgu")
        ah, al = split2(first[...])
        low2 = lax.dot_general(h0[QUADS * RF:, :], jnp.concatenate([ah, al], axis=0), nt, preferred_element_type=F32)
        low = low2[:, :RANK] + low2[:, RANK:]
        lh, ll = split2(low)
        low_s[...] = low
        low3[...] = jnp.concatenate([lh, ll, lh], axis=1)

    def spread_step():
        hid_t[...] = jnp.transpose(h0[QUADS * RF:, :])
        for q in range(QUADS):
            lq = low_s[q * RP:(q + 1) * RP, :]
            l1, l2 = split2(lq)
            l3 = (lq - l1.astype(F32) - l2.astype(F32)).astype(BF)
            s = lax.dot_general(jnp.concatenate([l1, l2, l3, jnp.zeros_like(l1)], axis=1), sel[q], tn,
                                preferred_element_type=F32)
            v = (s[0:RANK] + s[RANK:2 * RANK] + s[2 * RANK:3 * RANK]) * quad_row(kept["share"], q)
            hi, lo = split2(v)
            low_t[0:RANK, q * TOKQ:(q + 1) * TOKQ] = hi
            low_t[RANK:, q * TOKQ:(q + 1) * TOKQ] = lo

    def partial_step():
        r, i = next(kept["half"])
        at = pl.ds(pl.multiple_of(lax.rem(me.y + r + NX, NX) * COLS + i * CHUNK, CHUNK), CHUNK)

        def body(_, c):
            r0 = dot(h0[...], down[0, :, at])
            rp = r0[QUADS * RF:] + dot(low3[...], b3[:, at])
            r1 = dot(h1[...], down[1, :, at])
            for q in range(QUADS):
                rows[q, 0:RF] = r0[q * RF:(q + 1) * RF].astype(BF)
                rows[q, RF:RF + RP] = rp[q * RP:(q + 1) * RP].astype(BF)
                rows[q, RF + RP:] = r1[q * RF:(q + 1) * RF].astype(BF)
            for q in range(QUADS):
                tok[4 * q:4 * q + 4, :, at] = dot(wt[q], rows[q]).astype(BF).reshape(4, BLOCK, CHUNK)
            return c

        body(0, 0)

    got_b = {}

    def grad_step():
        i = next(kept["grad"])
        r = ROW_OF[i]
        res = big[i, :, 0:COLS]
        gb = dot(low_t[...], res)
        gbuf[i] = gb[:RANK] + gb[RANK:]
        tx.tag = "x"
        for dx in range(NX):
            if (dx, r) != (0, 0):
                block = lax.rem(me.x + dx, NX) * BLOCK
                got_b[dx, r] = tx.send(gbuf.at[i, :, pl.ds(pl.multiple_of(block, BLOCK), BLOCK)],
                                       rb.at[i * NX + dx], me.dev_xy(dx, r))
        v = lax.dot_general(b3[RANK:, stripe(r)], res, nt, preferred_element_type=F32)
        bt[...] = v if i == 0 else bt[...] + v

    steps = {"T": table_step, "Q": gather_step, "E": row0_step, "F": rows1_step, "L": last0_step, "l": last1_step,
             "W": low_step, "V": spread_step, "P": partial_step, "C": grad_step}
    for op in "".join(PLAN):
        if op in steps:
            steps[op]()
        else:
            tx.tag = op
            for j in jobs[op]:
                next(j)

    na = HIDDEN // GROUP
    for q in range(QUADS):
        at = slice(q * TOKQ, (q + 1) * TOKQ)
        v = (bt[:RANK, at] + bt[RANK:, at]) * quad_row(kept["share"], q)
        hi, lo = split2(v)
        picked = lax.dot_general(sel[q], jnp.concatenate([hi, lo], axis=0), nt, preferred_element_type=F32)
        back[q * RP:(q + 1) * RP, :] = picked.astype(BF)
    ga = dot(hid_t[...], back[...])
    gabuf[...] = ga[:, :RANK] + ga[:, RANK:]
    tx.tag = "x"
    got_a = {}
    for i, (dx, dy) in enumerate(peers):
        if (dx, dy) != (0, 0):
            lo = pl.multiple_of(me.xy(dx, dy) * na, na)
            got_a[dx, dy] = tx.send(gabuf.at[pl.ds(lo, na)], ra.at[i], me.dev_xy(dx, dy))
    tb = gbuf[0, :, pl.ds(pl.multiple_of(me.x * BLOCK, BLOCK), BLOCK)]
    for i, p in enumerate(peers):
        if p != (0, 0):
            tx.arrived(got_b[p], rb.at[i], me.dev_xy(*p))
            tb = tb + rb[i]
    gb_o[...] = tb
    ta = gabuf[pl.ds(pl.multiple_of(me.dp * na, na), na), :]
    for i, p in enumerate(peers):
        if p != (0, 0):
            tx.arrived(got_a[p], ra.at[i], me.dev_xy(*p))
            ta = ta + ra[i]
    ga_o[...] = ta
    assert tx.count == SENDS
    tx.drain("mtgud0123x")


def main_call(gate, up, down, tok, fid, pid, fsc, psc, first, second):
    sds = jax.ShapeDtypeStruct
    vm = pltpu.VMEM
    na, nb = HIDDEN // GROUP, WIDTH // GROUP
    return pl.pallas_call(
        main_kernel,
        out_shape=(sds((na, RANK), F32), sds((RANK, nb), F32)),
        in_specs=[ANY] * 4 + [VM] * 6,
        out_specs=(VM, VM),
        scratch_shapes=[
            vm((4, WIDTH, HIDDEN), BF), vm((2, HIDDEN, WIDTH), BF),
            vm((GROUP, BLOCK, WIDTH), BF), vm((GROUP, 16, BLOCK), F32),
            vm((ROWS0, WIDTH), BF), vm((ROWS1, WIDTH), BF), vm((2, ROWS0 + ROWS1, HIDDEN), F32),
            vm((ROWS0, HIDDEN), BF), vm((ROWS1, HIDDEN), BF),
            vm((QUADS, TOKQ, RQ), BF), vm((QUADS * RP, RANK), F32), vm((QUADS * RP, 3 * RANK), BF),
            vm((3 * RANK, WIDTH), BF), vm((QUADS, RQ, CHUNK), BF),
            vm((STRIPES, NZ, BLOCK, COLS), BF), vm((STRIPES, 14, BLOCK // 2, COLS), BF),
            vm((QUADS, RP, TOKQ), BF), vm((2 * RANK, GROUP * BLOCK), BF), vm((2 * RANK, GROUP * BLOCK), F32),
            vm((HIDDEN, QUADS * RP), BF), vm((QUADS * RP, 2 * RANK), BF), vm((STRIPES, RANK, COLS), F32),
            vm((HIDDEN, RANK), F32), vm((GROUP, na, RANK), F32), vm((GROUP, RANK, nb), F32),
            pltpu.SemaphoreType.DMA((SENDS,)), pltpu.SemaphoreType.DMA((SENDS,)), pltpu.SemaphoreType.DMA((4,)),
        ],
        compiler_params=pltpu.CompilerParams(collective_id=0, has_side_effects=True, vmem_limit_bytes=63 << 20),
        name="main",
    )(gate, up, down, tok, fid, pid, fsc, psc, first, second)


def shards(tokens, fid, pid, fsc, psc, gate, up, down, first, second):
    ga, gb = main_call(gate, up, down, tokens, fid.T, pid.T, fsc.T, psc.T, first[0].T, second)
    return ga[None], gb[None]


def solution(mesh):
    rows = P(("dp", "expert"), None)
    return jax.shard_map(
        shards,
        mesh=mesh,
        in_specs=(rows,) * 5 + (P("expert", "dp", None), P("expert", "dp", None), P("expert", None, "dp"),
                                P("expert", None, None), P("expert", None, None)),
        out_specs=(P("expert", "dp", None), P("expert", None, "dp")),
        check_vma=False,
    )
```

time: 245 us -> 212 us (0.87)
  Pallas kernels: 236 us -> 209 us
  other arithmetic: 4.08 us -> 0 us
  local copies, waits for them, and re-layouts: 4.6 us -> 1.97 us
    pallas_call x3 -> x1, Pallas kernels: 236 us -> 209 us  [main_call(): pl.pallas_call(main_kernel, out_shape=(sds((na, RANK), F32), sds((RANK, n...]
    unnamed x3 -> x4, local copies, waits for them, and re-layouts: 4.6 us -> 1.97 us
where the time goes in v3:
time: 212 us
  Pallas kernels  209 us (99%)
    pallas_call x1, Pallas kernels, main_call(): pl.pallas_call(main_kernel, out_shape=(sds((na, RANK), F32), sds((RANK, n...  209 us

profile of v3, /device:TPU:1, one launch (start us, length us, event | category | flops | bytes accessed | tf_op | source)
XLA Modules:
  0.0 211.7 jit_solution(3032417031451230916)
XLA Ops:
  0.6 209.0 %main.1 = (f32[48,64]{1,0:T(8,128)}, f32[64,128]{1,0:T(8,128)}) custom-call(bf16[2,128,768]{2,1,0:T(8,128)(2,1)} %gate_i.1, bf16[2,128,768]{2,1,0:T(8,128)(2,1)} %up_i.1, bf16[2,768,128]{2,1,0:T(8,128)(2,1)} %down_i.1, bf16[128,2048]{1,0:T(8,128)(2,1)} %tok_i.1, s32[4,128]{1,0:T(4,128)} %bitcast.12, s32[4,128]{1,0:T(4,128)} %bitcast.13, f32[4,128]{1,0:T(4,128)} %bitcast.14, ...), custom_call_target="tpu_custom_call" | custom-call | tf_op jit(solution)/shard_map/main/pallas_call | solution.py:542
  209.7 0.0 copy-start
  209.7 1.4 copy.14
  211.1 0.0 copy-done
  211.1 0.6 copy.15
Async XLA Ops:
  209.7 1.4 copy-start

commit v4 on v3

--- a/solution.py
+++ b/solution.py
@@ -122,22 +122,25 @@
 
 
 def gather_xy(me, tx, own, region, x_first):
-    def idx(p, q):
-        return me.xy(p, q) if x_first else me.xy(q, p)
+    def at(p, q):
+        return (p, q) if x_first else (q, p)
+
+    def reg(p, q, h, dp_=0, dq_=0):
+        return region(*at(p, q), h, *at(dp_, dq_))
 
     def dev(p, q):
-        return me.dev_xy(p, q) if x_first else me.dev_xy(q, p)
+        return me.dev_xy(*at(p, q))
 
     def src(p, q, h):
-        return own(h) if (p, q) == (0, 0) else region(idx(p, q), h)
+        return own(h) if (p, q) == (0, 0) else reg(p, q, h)
 
     def ring(p, q, dp_, dq_):
-        return (tx.send(src(p, q, None), region(idx(p, q), None), dev(dp_, dq_)),
-                tx.send(src(p, q, None), region(idx(p, q), None), dev(-dp_, -dq_)))
+        return (tx.send(src(p, q, None), reg(p, q, None, dp_, dq_), dev(dp_, dq_)),
+                tx.send(src(p, q, None), reg(p, q, None, -dp_, -dq_), dev(-dp_, -dq_)))
 
     def relay(n, p, q, dp_, dq_, h):
-        tx.arrived(n, region(idx(p, q), None), dev(dp_, dq_))
-        return tx.send(region(idx(p, q), h), region(idx(p, q), h), dev(dp_, dq_))
+        tx.arrived(n, reg(p, q, None), dev(dp_, dq_))
+        return tx.send(reg(p, q, h), reg(p, q, h, dp_, dq_), dev(dp_, dq_))
 
     far = {}
 
@@ -147,7 +150,7 @@
 
     def opposite(p):
         for h in (0, 1):
-            tx.arrived(far[p][h], region(idx(p, 2), h), dev(0, 1))
+            tx.arrived(far[p][h], reg(p, 2, h), dev(0, 1))
 
     first = ring(0, 0, 1, 0)
     second = {0: ring(0, 0, 0, 1)}
@@ -159,24 +162,21 @@
     yield
     along_q(0)
     yield
-    tx.arrived(o0, region(idx(2, 0), 0), dev(1, 0))
-    tx.arrived(o1, region(idx(2, 0), 1), dev(-1, 0))
+    tx.arrived(o0, reg(2, 0, 0), dev(1, 0))
+    tx.arrived(o1, reg(2, 0, 1), dev(-1, 0))
     second[2] = ring(2, 0, 0, 1)
     yield
-    if not x_first:
-        opposite(0)
+    opposite(0)
     yield
     along_q(-1)
     along_q(1)
     yield
     along_q(2)
     yield
-    if not x_first:
-        opposite(-1)
-        opposite(1)
-    yield
-    for p in (0, -1, 1, 2) if x_first else (2,):
-        opposite(p)
+    opposite(-1)
+    opposite(1)
+    yield
+    opposite(2)
     yield
 
 
@@ -228,19 +228,24 @@
     return jnp.where(slot == pos, share, 0.0)
 
 
-STRIPES = 4
-COLS = WIDTH // STRIPES
-ROW_OF = (0, -1, 1, 2)
+COLS = WIDTH // NX
+NEAR = ((0, 0), (1, 0), (-1, 0), (0, 1), (0, -1), (2, 0), (0, 2), (1, 1), (1, -1), (-1, 1), (-1, -1),
+        (2, 1), (2, -1), (1, 2), (-1, 2), (2, 2))
+CUTS = (0, 1, 3, 5, 9, 13, 16)
+STEPS_P = ((0, 1), (1, 3), (3, 5), (5, 7), (7, 9), (9, 11), (11, 13), (13, 15), (15, 16))
+PARTS = ((0, 5), (5, 9), (9, 13), (13, 16))
+STRIPES = len(CUTS) - 1
 ORDER = (4, 3, -3, 2, -2, 1, -1, 0)
 SENDS = 6 * 20 + 2 * 17 + STRIPES * (8 + 14 + 17) + 2 * (GROUP - 1)
 
 PLAN = (
-    "gummttdgugmmtmtutgmTgutgguQQQQugEgududFuLlWdddPP00dd0P0P101d",
-    "0P101P201P21P32013231023132V130231C232C3232C3C",
+    "umtmgutgmutmgutgmugmTugtutQQQgdQEguFguLlWPd0dP101P201212012d",
+    "0dP1d2P301d3P2d1Pd403P434P2505145315043024V253504352452314C5",
+    "334C54C5C",
 )
 
 
-def reduce_stripe(me, tx, ci, cols, part, theirs, ring, out):
+def reduce_stripe(me, tx, cols, part, theirs, ring, out):
     half = BLOCK // 2
 
     def mine(k, h=None):
@@ -250,16 +255,16 @@
     def region(z, c, h):
         lo = (z * 2 + c) * BLOCK
         if h is None:
-            return out.at[ci, pl.ds(pl.multiple_of(lo, BLOCK), BLOCK), 0:COLS]
-        return out.at[ci, pl.ds(pl.multiple_of(lo + h * half, half), half), 0:COLS]
-
-    swap = {k: tx.send(part.at[me.zz(k) * 2 + 1 - me.c, :, cols], theirs.at[ci, me.zz(k)], me.partner()) for k in ORDER}
+            return out.at[pl.ds(pl.multiple_of(lo, BLOCK), BLOCK), :]
+        return out.at[pl.ds(pl.multiple_of(lo + h * half, half), half), :]
+
+    swap = {k: tx.send(part.at[me.zz(k) * 2 + 1 - me.c, :, cols], theirs.at[me.zz(k)], me.partner()) for k in ORDER}
     yield
 
     def pair_sum(k):
-        tx.arrived(swap[k], theirs.at[ci, me.zz(k)], me.partner())
+        tx.arrived(swap[k], theirs.at[me.zz(k)], me.partner())
         r = mine(k)
-        r[...] = (r[...].astype(F32) + theirs[ci, me.zz(k)].astype(F32)).astype(BF)
+        r[...] = (r[...].astype(F32) + theirs[me.zz(k)].astype(F32)).astype(BF)
 
     slot, waiting = {}, {}
 
@@ -267,10 +272,10 @@
         r = mine(sign * j, h)
         if (sign, h) in waiting:
             n, s = waiting[(sign, h)]
-            tx.arrived(n, ring.at[ci, s], me.dev_z(sign))
-            r[...] = (r[...].astype(F32) + ring[ci, s].astype(F32)).astype(BF)
+            tx.arrived(n, ring.at[s], me.dev_z(sign))
+            r[...] = (r[...].astype(F32) + ring[s].astype(F32)).astype(BF)
         s = slot.setdefault((sign, h, j), len(slot))
-        waiting[(sign, h)] = (tx.send(r, ring.at[ci, s], me.dev_z(sign)), s)
+        waiting[(sign, h)] = (tx.send(r, ring.at[s], me.dev_z(sign)), s)
 
     pair_sum(4)
     push(1, 0, 4)
@@ -294,8 +299,8 @@
         total = mine(0, h)[...].astype(F32)
         for sign in (1, -1):
             n, s = waiting[(sign, h)]
-            tx.arrived(n, ring.at[ci, s], me.dev_z(sign))
-            total = total + ring[ci, s].astype(F32)
+            tx.arrived(n, ring.at[s], me.dev_z(sign))
+            total = total + ring[s].astype(F32)
         region(me.z, me.c, h)[...] = total.astype(BF)
     yield from gather_z(me, tx, region(me.z, me.c, None), region)
 
@@ -309,12 +314,11 @@
     loads = [
         pltpu.make_async_copy(s, d, loc_sem.at[i]) for i, (s, d) in enumerate((
             (tok_i, tok.at[me.ex]), (gate_i, big.at[0:2, mine, :]),
-            (up_i, big.at[2:4, mine, :]), (down_i, down.at[:, :, mine])))
+            (up_i, big.at[2:4, mine, :]), (down_i, down.at[:, :, 0:BLOCK])))
     ]
     for cp in loads:
         cp.start()
-    peers = [(dx, dy) for dy in ROW_OF for dx in range(NX)]
-    barrier([me.dev_xy(*p) for p in peers if p != (0, 0)] + [me.dev_z(1), me.dev_z(-1), me.partner()])
+    barrier([me.dev_xy(*p) for p in NEAR[1:]] + [me.dev_z(1), me.dev_z(-1), me.partner()])
 
     def block_region(ref, size):
         def region(z, c, h):
@@ -323,7 +327,8 @@
         return region
 
     def rows_region(i):
-        def region(dp, h):
+        def region(dx, dy, h, ex, ey):
+            dp = me.xy(dx, dy)
             if h is None:
                 return big.at[i, pl.ds(pl.multiple_of(dp * BLOCK, BLOCK), BLOCK), :]
             n = BLOCK // 2
@@ -331,11 +336,10 @@
         return region
 
     def cols_region(e):
-        def region(dp, h):
-            cols = pl.ds(pl.multiple_of(dp * BLOCK, BLOCK), BLOCK)
-            if h is None:
-                return down.at[e, :, cols]
-            return down.at[e, pl.ds(h * (HIDDEN // 2), HIDDEN // 2), cols]
+        def region(dx, dy, h, ex, ey):
+            j = [(a % NX, b % NX) for a, b in NEAR].index(((dx - ex) % NX, (dy - ey) % NX))
+            rows_h = slice(None) if h is None else pl.ds(h * (HIDDEN // 2), HIDDEN // 2)
+            return down.at[e, rows_h, j * BLOCK:(j + 1) * BLOCK]
         return region
 
     def own_half(ref, e):
@@ -355,8 +359,15 @@
         "u": [gather_xy(me, tx, own_half(up_i, e), rows_region(2 + e), e == 0) for e in (0, 1)],
         "d": [gather_xy(me, tx, own_half(down_i, e), cols_region(e), e == 0) for e in (0, 1)],
     }
-    for i, r in enumerate(ROW_OF):
-        jobs[str(i)] = [reduce_stripe(me, tx, i, stripe(r), tok, theirs, ring, big)]
+    def span(lo, hi):
+        return slice(lo * BLOCK, hi * BLOCK)
+
+    for i in range(STRIPES):
+        lo, hi = CUTS[i], CUTS[i + 1]
+        home = [k for k, (a, b) in enumerate(PARTS) if a <= lo < b][0]
+        base = PARTS[home][0]
+        jobs[str(i)] = [reduce_stripe(me, tx, span(lo, hi), tok, theirs.at[:, :, span(lo, hi)], ring.at[:, :, span(lo, hi)],
+                                      big.at[home, :, span(lo - base, hi - base)])]
 
     fsc, psc = fsc_i[...], psc_i[...]
     meta[me.ex] = jnp.concatenate([
@@ -367,8 +378,9 @@
     def table_step():
         for cp in loads:
             cp.wait()
-        bh, bl = split2(second[0])
-        b3[0:RANK], b3[RANK:2 * RANK], b3[2 * RANK:] = bh, bh, bl
+        for j, off in enumerate(NEAR):
+            bh, bl = split2(second[0, :, pl.ds(pl.multiple_of(me.xy(*off) * BLOCK, BLOCK), BLOCK)])
+            b3[:, span(j, j + 1)] = jnp.concatenate([bh, bh, bl], axis=0)
         (pa, wa), (pb, wb), (pp, wp) = tables(meta[...])
         turned = jnp.transpose(jnp.concatenate([pa, pb, pp, -wa, -wb, wp, pp, wp], axis=0))
         for q in range(QUADS):
@@ -380,8 +392,8 @@
         kept["rows"] = (pa, pb, pp)
         kept["share"] = wp
         kept["quad"] = iter(range(QUADS))
-        kept["half"] = iter([(r, i) for r in ROW_OF for i in range(COLS // CHUNK)])
-        kept["grad"] = iter(range(STRIPES))
+        kept["part"] = iter(STEPS_P)
+        kept["grad"] = iter(range(len(PARTS)))
 
     def gather_step():
         q = next(kept["quad"])
@@ -460,38 +472,30 @@
             low_t[RANK:, q * TOKQ:(q + 1) * TOKQ] = lo
 
     def partial_step():
-        r, i = next(kept["half"])
-        at = pl.ds(pl.multiple_of(lax.rem(me.y + r + NX, NX) * COLS + i * CHUNK, CHUNK), CHUNK)
-
-        def body(_, c):
-            r0 = dot(h0[...], down[0, :, at])
-            rp = r0[QUADS * RF:] + dot(low3[...], b3[:, at])
-            r1 = dot(h1[...], down[1, :, at])
-            for q in range(QUADS):
-                rows[q, 0:RF] = r0[q * RF:(q + 1) * RF].astype(BF)
-                rows[q, RF:RF + RP] = rp[q * RP:(q + 1) * RP].astype(BF)
-                rows[q, RF + RP:] = r1[q * RF:(q + 1) * RF].astype(BF)
-            for q in range(QUADS):
-                tok[4 * q:4 * q + 4, :, at] = dot(wt[q], rows[q]).astype(BF).reshape(4, BLOCK, CHUNK)
-            return c
-
-        body(0, 0)
+        at = span(*next(kept["part"]))
+        n = at.stop - at.start
+        r0 = dot(h0[...], down[0, :, at])
+        rp = r0[QUADS * RF:] + dot(low3[...], b3[:, at])
+        r1 = dot(h1[...], down[1, :, at])
+        for q in range(QUADS):
+            rows[q, 0:RF, 0:n] = r0[q * RF:(q + 1) * RF].astype(BF)
+            rows[q, RF:RF + RP, 0:n] = rp[q * RP:(q + 1) * RP].astype(BF)
+            rows[q, RF + RP:, 0:n] = r1[q * RF:(q + 1) * RF].astype(BF)
+        for q in range(QUADS):
+            tok[4 * q:4 * q + 4, :, at] = dot(wt[q], rows[q, :, 0:n]).astype(BF).reshape(4, BLOCK, n)
 
     got_b = {}
 
     def grad_step():
         i = next(kept["grad"])
-        r = ROW_OF[i]
-        res = big[i, :, 0:COLS]
+        lo, hi = PARTS[i]
+        res = big[i, :, 0:(hi - lo) * BLOCK]
         gb = dot(low_t[...], res)
-        gbuf[i] = gb[:RANK] + gb[RANK:]
+        gbuf[:, span(lo, hi)] = gb[:RANK] + gb[RANK:]
         tx.tag = "x"
-        for dx in range(NX):
-            if (dx, r) != (0, 0):
-                block = lax.rem(me.x + dx, NX) * BLOCK
-                got_b[dx, r] = tx.send(gbuf.at[i, :, pl.ds(pl.multiple_of(block, BLOCK), BLOCK)],
-                                       rb.at[i * NX + dx], me.dev_xy(dx, r))
-        v = lax.dot_general(b3[RANK:, stripe(r)], res, nt, preferred_element_type=F32)
+        for j in range(max(lo, 1), hi):
+            got_b[j] = tx.send(gbuf.at[:, span(j, j + 1)], rb.at[j], me.dev_xy(*NEAR[j]))
+        v = lax.dot_general(b3[RANK:, span(lo, hi)], res, nt, preferred_element_type=F32)
         bt[...] = v if i == 0 else bt[...] + v
 
     steps = {"T": table_step, "Q": gather_step, "E": row0_step, "F": rows1_step, "L": last0_step, "l": last1_step,
@@ -515,24 +519,21 @@
     gabuf[...] = ga[:, :RANK] + ga[:, RANK:]
     tx.tag = "x"
     got_a = {}
-    for i, (dx, dy) in enumerate(peers):
-        if (dx, dy) != (0, 0):
-            lo = pl.multiple_of(me.xy(dx, dy) * na, na)
-            got_a[dx, dy] = tx.send(gabuf.at[pl.ds(lo, na)], ra.at[i], me.dev_xy(dx, dy))
-    tb = gbuf[0, :, pl.ds(pl.multiple_of(me.x * BLOCK, BLOCK), BLOCK)]
-    for i, p in enumerate(peers):
-        if p != (0, 0):
-            tx.arrived(got_b[p], rb.at[i], me.dev_xy(*p))
-            tb = tb + rb[i]
+    for j in range(1, GROUP):
+        lo = pl.multiple_of(me.xy(*NEAR[j]) * na, na)
+        got_a[j] = tx.send(gabuf.at[pl.ds(lo, na)], ra.at[j], me.dev_xy(*NEAR[j]))
+    tb = gbuf[:, 0:BLOCK]
+    for j in range(1, GROUP):
+        tx.arrived(got_b[j], rb.at[j], me.dev_xy(*NEAR[j]))
+        tb = tb + rb[j]
     gb_o[...] = tb
     ta = gabuf[pl.ds(pl.multiple_of(me.dp * na, na), na), :]
-    for i, p in enumerate(peers):
-        if p != (0, 0):
-            tx.arrived(got_a[p], ra.at[i], me.dev_xy(*p))
-            ta = ta + ra[i]
+    for j in range(1, GROUP):
+        tx.arrived(got_a[j], ra.at[j], me.dev_xy(*NEAR[j]))
+        ta = ta + ra[j]
     ga_o[...] = ta
     assert tx.count == SENDS
-    tx.drain("mtgud0123x")
+    tx.drain("mtgud012345x")
 
 
 def main_call(gate, up, down, tok, fid, pid, fsc, psc, first, second):
@@ -551,9 +552,9 @@
             vm((ROWS0, HIDDEN), BF), vm((ROWS1, HIDDEN), BF),
             vm((QUADS, TOKQ, RQ), BF), vm((QUADS * RP, RANK), F32), vm((QUADS * RP, 3 * RANK), BF),
             vm((3 * RANK, WIDTH), BF), vm((QUADS, RQ, CHUNK), BF),
-            vm((STRIPES, NZ, BLOCK, COLS), BF), vm((STRIPES, 14, BLOCK // 2, COLS), BF),
+            vm((NZ, BLOCK, WIDTH), BF), vm((14, BLOCK // 2, WIDTH), BF),
             vm((QUADS, RP, TOKQ), BF), vm((2 * RANK, GROUP * BLOCK), BF), vm((2 * RANK, GROUP * BLOCK), F32),
-            vm((HIDDEN, QUADS * RP), BF), vm((QUADS * RP, 2 * RANK), BF), vm((STRIPES, RANK, COLS), F32),
+            vm((HIDDEN, QUADS * RP), BF), vm((QUADS * RP, 2 * RANK), BF), vm((RANK, WIDTH), F32),
             vm((HIDDEN, RANK), F32), vm((GROUP, na, RANK), F32), vm((GROUP, RANK, nb), F32),
             pltpu.SemaphoreType.DMA((SENDS,)), pltpu.SemaphoreType.DMA((SENDS,)), pltpu.SemaphoreType.DMA((4,)),
         ],

time: 212 us -> 197 us (0.929)
  Pallas kernels: 209 us -> 194 us
    pallas_call x1, Pallas kernels: 209 us -> 194 us  [main_call(): pl.pallas_call(main_kernel, out_shape=(sds((na, RANK), F32), sds((RANK, n...]
where the time goes in v4:
time: 197 us
  Pallas kernels  194 us (98%)
  local copies, waits for them, and re-layouts  1.97 us (1%)
    pallas_call x1, Pallas kernels, main_call(): pl.pallas_call(main_kernel, out_shape=(sds((na, RANK), F32), sds((RANK, n...  194 us

profile of v4, /device:TPU:1, one launch (start us, length us, event | category | flops | bytes accessed | tf_op | source)
XLA Modules:
  0.0 196.5 jit_solution(2122427017677616515)
XLA Ops:
  0.6 193.9 %main.1 = (f32[48,64]{1,0:T(8,128)}, f32[64,128]{1,0:T(8,128)}) custom-call(bf16[2,128,768]{2,1,0:T(8,128)(2,1)} %gate_i.1, bf16[2,128,768]{2,1,0:T(8,128)(2,1)} %up_i.1, bf16[2,768,128]{2,1,0:T(8,128)(2,1)} %down_i.1, bf16[128,2048]{1,0:T(8,128)(2,1)} %tok_i.1, s32[4,128]{1,0:T(4,128)} %bitcast.12, s32[4,128]{1,0:T(4,128)} %bitcast.13, f32[4,128]{1,0:T(4,128)} %bitcast.14, ...), custom_call_target="tpu_custom_call" | custom-call | tf_op jit(solution)/shard_map/main/pallas_call | solution.py:543
  194.6 0.0 copy-start
  194.6 1.4 copy.14
  195.9 0.0 copy-done
  195.9 0.6 copy.15
Async XLA Ops:
  194.6 1.4 copy-start

commit v5 on v4

--- a/solution.py
+++ b/solution.py
@@ -239,9 +239,9 @@
 SENDS = 6 * 20 + 2 * 17 + STRIPES * (8 + 14 + 17) + 2 * (GROUP - 1)
 
 PLAN = (
-    "umtmgutgmutmgutgmugmTugtutQQQgdQEguFguLlWPd0dP101P201212012d",
-    "0dP1d2P301d3P2d1Pd403P434P2505145315043024V253504352452314C5",
-    "334C54C5C",
+    "gmtmuggtuumtmtggugmmuTugttQQQQEueudgFgfuGLlWP00ddP101P021210",
+    "210d2dP01d2P0313Pd1d2P34421d3P4P552051405354523V52434034215C",
+    "345334C54C5C",
 )
 
 
@@ -318,6 +318,10 @@
     ]
     for cp in loads:
         cp.start()
+    fsc, psc = fsc_i[...], psc_i[...]
+    meta[me.ex] = jnp.concatenate([
+        fid_i[...].astype(F32), pid_i[...].astype(F32),
+        fsc / jnp.sum(fsc, axis=0, keepdims=True), psc / jnp.sum(psc, axis=0, keepdims=True)], axis=0)
     barrier([me.dev_xy(*p) for p in NEAR[1:]] + [me.dev_z(1), me.dev_z(-1), me.partner()])
 
     def block_region(ref, size):
@@ -369,10 +373,6 @@
         jobs[str(i)] = [reduce_stripe(me, tx, span(lo, hi), tok, theirs.at[:, :, span(lo, hi)], ring.at[:, :, span(lo, hi)],
                                       big.at[home, :, span(lo - base, hi - base)])]
 
-    fsc, psc = fsc_i[...], psc_i[...]
-    meta[me.ex] = jnp.concatenate([
-        fid_i[...].astype(F32), pid_i[...].astype(F32),
-        fsc / jnp.sum(fsc, axis=0, keepdims=True), psc / jnp.sum(psc, axis=0, keepdims=True)], axis=0)
     kept = {}
 
     def table_step():
@@ -411,7 +411,7 @@
 
         lax.fori_loop(0, 4, body, 0)
 
-    def product(x, e, m, first_row, parts, how, h=None):
+    def product(x, e, m, first_row, w, parts, h=None):
         rows_m = x.shape[0] // m
 
         def body(i, _):
@@ -419,32 +419,29 @@
             rr = pl.ds(lo, rows_m)
             ra_ = pl.ds(first_row + lo, rows_m)
             cc = pl.ds(pl.multiple_of(lax.div(i, m) * CHUNK, CHUNK), CHUNK)
-            out = []
-            for w in (0, 1):
-                v = sum(dot(x[rr, stripe(r)], big[2 * w + e, stripe(r), cc]) for r in parts)
-                out.append(v if how == "set" else acc[w, ra_, cc] + v)
-            if how == "end":
-                g, u = out
-                h[rr, cc] = (g / (1.0 + jnp.exp(-g)) * u).astype(BF)
+            v = sum(dot(x[rr, stripe(r)], big[2 * w + e, stripe(r), cc]) for r in parts)
+            if parts != (0,):
+                v = acc[w, ra_, cc] + v
+            if h is None:
+                acc[w, ra_, cc] = v
             else:
-                acc[0, ra_, cc], acc[1, ra_, cc] = out
+                g = acc[0, ra_, cc]
+                h[rr, cc] = (g / (1.0 + jnp.exp(-g)) * v).astype(BF)
             return 0
 
         lax.fori_loop(0, m * (HIDDEN // CHUNK), body, 0)
 
-    def row0_step():
-        product(x0, 0, 2, 0, (0,), "set")
-        product(x1, 1, 1, ROWS0, (0,), "set")
-
-    def rows1_step():
-        product(x0, 0, 2, 0, (-1, 1), "add")
-        product(x1, 1, 1, ROWS0, (-1, 1), "add")
+    def both(w, parts):
+        def step_of():
+            product(x0, 0, 2, 0, w, parts)
+            product(x1, 1, 1, ROWS0, w, parts)
+        return step_of
 
     def last0_step():
-        product(x0, 0, 2, 0, (2,), "end", h0)
+        product(x0, 0, 2, 0, 1, (2,), h0)
 
     def last1_step():
-        product(x1, 1, 1, ROWS0, (2,), "end", h1)
+        product(x1, 1, 1, ROWS0, 1, (2,), h1)
 
     nt = (((1,), (1,)), ((), ()))
     tn = (((0,), (0,)), ((), ()))
@@ -486,19 +483,24 @@
 
     got_b = {}
 
+    def grad_b(i):
+        lo, hi = PARTS[i]
+        gb = dot(low_t[...], big[i, :, 0:(hi - lo) * BLOCK])
+        gbuf[:, span(lo, hi)] = gb[:RANK] + gb[RANK:]
+        tx.tag = "x"
+        for j in reversed(range(max(lo, 1), hi)):
+            got_b[j] = tx.send(gbuf.at[:, span(j, j + 1)], rb.at[j], me.dev_xy(*NEAR[j]))
+
     def grad_step():
         i = next(kept["grad"])
         lo, hi = PARTS[i]
-        res = big[i, :, 0:(hi - lo) * BLOCK]
-        gb = dot(low_t[...], res)
-        gbuf[:, span(lo, hi)] = gb[:RANK] + gb[RANK:]
-        tx.tag = "x"
-        for j in range(max(lo, 1), hi):
-            got_b[j] = tx.send(gbuf.at[:, span(j, j + 1)], rb.at[j], me.dev_xy(*NEAR[j]))
-        v = lax.dot_general(b3[RANK:, span(lo, hi)], res, nt, preferred_element_type=F32)
+        v = lax.dot_general(b3[RANK:, span(lo, hi)], big[i, :, 0:(hi - lo) * BLOCK], nt, preferred_element_type=F32)
         bt[...] = v if i == 0 else bt[...] + v
-
-    steps = {"T": table_step, "Q": gather_step, "E": row0_step, "F": rows1_step, "L": last0_step, "l": last1_step,
+        if i < len(PARTS) - 1:
+            grad_b(i)
+
+    steps = {"T": table_step, "Q": gather_step, "E": both(0, (0,)), "e": both(1, (0,)), "F": both(0, (-1, 1)),
+             "f": both(1, (-1, 1)), "G": both(0, (2,)), "L": last0_step, "l": last1_step,
              "W": low_step, "V": spread_step, "P": partial_step, "C": grad_step}
     for op in "".join(PLAN):
         if op in steps:
@@ -519,9 +521,10 @@
     gabuf[...] = ga[:, :RANK] + ga[:, RANK:]
     tx.tag = "x"
     got_a = {}
-    for j in range(1, GROUP):
+    for j in reversed(range(1, GROUP)):
         lo = pl.multiple_of(me.xy(*NEAR[j]) * na, na)
         got_a[j] = tx.send(gabuf.at[pl.ds(lo, na)], ra.at[j], me.dev_xy(*NEAR[j]))
+    grad_b(len(PARTS) - 1)
     tb = gbuf[:, 0:BLOCK]
     for j in range(1, GROUP):
         tx.arrived(got_b[j], rb.at[j], me.dev_xy(*NEAR[j]))

time: 197 us -> 202 us (1.025)
  Pallas kernels: 194 us -> 199 us
    pallas_call x1, Pallas kernels: 194 us -> 199 us  [main_call(): pl.pallas_call(main_kernel, out_shape=(sds((na, RANK), F32), sds((RANK, n...]
where the time goes in v5:
time: 202 us
  Pallas kernels  199 us (99%)
    pallas_call x1, Pallas kernels, main_call(): pl.pallas_call(main_kernel, out_shape=(sds((na, RANK), F32), sds((RANK, n...  199 us

profile of v5, /device:TPU:1, one launch (start us, length us, event | category | flops | bytes accessed | tf_op | source)
XLA Modules:
  0.0 201.5 jit_solution(2269664226673668270)
XLA Ops:
  0.6 198.9 %main.1 = (f32[48,64]{1,0:T(8,128)}, f32[64,128]{1,0:T(8,128)}) custom-call(bf16[2,128,768]{2,1,0:T(8,128)(2,1)} %gate_i.1, bf16[2,128,768]{2,1,0:T(8,128)(2,1)} %up_i.1, bf16[2,768,128]{2,1,0:T(8,128)(2,1)} %down_i.1, bf16[128,2048]{1,0:T(8,128)(2,1)} %tok_i.1, s32[4,128]{1,0:T(4,128)} %bitcast.12, s32[4,128]{1,0:T(4,128)} %bitcast.13, f32[4,128]{1,0:T(4,128)} %bitcast.14, ...), custom_call_target="tpu_custom_call" | custom-call | tf_op jit(solution)/shard_map/main/pallas_call | solution.py:546
  199.6 0.0 copy-start
  199.6 1.4 copy.14
  200.9 0.0 copy-done
  200.9 0.6 copy.15
Async XLA Ops:
  199.6 1.4 copy-start

commit v6 on v4

--- a/solution.py
+++ b/solution.py
@@ -318,6 +318,10 @@
     ]
     for cp in loads:
         cp.start()
+    fsc, psc = fsc_i[...], psc_i[...]
+    meta[me.ex] = jnp.concatenate([
+        fid_i[...].astype(F32), pid_i[...].astype(F32),
+        fsc / jnp.sum(fsc, axis=0, keepdims=True), psc / jnp.sum(psc, axis=0, keepdims=True)], axis=0)
     barrier([me.dev_xy(*p) for p in NEAR[1:]] + [me.dev_z(1), me.dev_z(-1), me.partner()])
 
     def block_region(ref, size):
@@ -369,10 +373,6 @@
         jobs[str(i)] = [reduce_stripe(me, tx, span(lo, hi), tok, theirs.at[:, :, span(lo, hi)], ring.at[:, :, span(lo, hi)],
                                       big.at[home, :, span(lo - base, hi - base)])]
 
-    fsc, psc = fsc_i[...], psc_i[...]
-    meta[me.ex] = jnp.concatenate([
-        fid_i[...].astype(F32), pid_i[...].astype(F32),
-        fsc / jnp.sum(fsc, axis=0, keepdims=True), psc / jnp.sum(psc, axis=0, keepdims=True)], axis=0)
     kept = {}
 
     def table_step():
@@ -486,17 +486,21 @@
 
     got_b = {}
 
+    def grad_b(i):
+        lo, hi = PARTS[i]
+        gb = dot(low_t[...], big[i, :, 0:(hi - lo) * BLOCK])
+        gbuf[:, span(lo, hi)] = gb[:RANK] + gb[RANK:]
+        tx.tag = "x"
+        for j in reversed(range(max(lo, 1), hi)):
+            got_b[j] = tx.send(gbuf.at[:, span(j, j + 1)], rb.at[j], me.dev_xy(*NEAR[j]))
+
     def grad_step():
         i = next(kept["grad"])
         lo, hi = PARTS[i]
-        res = big[i, :, 0:(hi - lo) * BLOCK]
-        gb = dot(low_t[...], res)
-        gbuf[:, span(lo, hi)] = gb[:RANK] + gb[RANK:]
-        tx.tag = "x"
-        for j in range(max(lo, 1), hi):
-            got_b[j] = tx.send(gbuf.at[:, span(j, j + 1)], rb.at[j], me.dev_xy(*NEAR[j]))
-        v = lax.dot_general(b3[RANK:, span(lo, hi)], res, nt, preferred_element_type=F32)
+        v = lax.dot_general(b3[RANK:, span(lo, hi)], big[i, :, 0:(hi - lo) * BLOCK], nt, preferred_element_type=F32)
         bt[...] = v if i == 0 else bt[...] + v
+        if i < len(PARTS) - 1:
+            grad_b(i)
 
     steps = {"T": table_step, "Q": gather_step, "E": row0_step, "F": rows1_step, "L": last0_step, "l": last1_step,
              "W": low_step, "V": spread_step, "P": partial_step, "C": grad_step}
@@ -519,9 +523,10 @@
     gabuf[...] = ga[:, :RANK] + ga[:, RANK:]
     tx.tag = "x"
     got_a = {}
-    for j in range(1, GROUP):
+    for j in reversed(range(1, GROUP)):
         lo = pl.multiple_of(me.xy(*NEAR[j]) * na, na)
         got_a[j] = tx.send(gabuf.at[pl.ds(lo, na)], ra.at[j], me.dev_xy(*NEAR[j]))
+    grad_b(len(PARTS) - 1)
     tb = gbuf[:, 0:BLOCK]
     for j in range(1, GROUP):
         tx.arrived(got_b[j], rb.at[j], me.dev_xy(*NEAR[j]))

time: 197 us -> 198 us (level)
  Pallas kernels: 194 us -> 196 us
where the time goes in v6:
time: 198 us
  Pallas kernels  196 us (99%)
    pallas_call x1, Pallas kernels, main_call(): pl.pallas_call(main_kernel, out_shape=(sds((na, RANK), F32), sds((RANK, n...  196 us

profile of v6, /device:TPU:1, one launch (start us, length us, event | category | flops | bytes accessed | tf_op | source)
XLA Modules:
  0.0 198.2 jit_solution(444864583090435831)
XLA Ops:
  0.6 195.6 %main.1 = (f32[48,64]{1,0:T(8,128)}, f32[64,128]{1,0:T(8,128)}) custom-call(bf16[2,128,768]{2,1,0:T(8,128)(2,1)} %gate_i.1, bf16[2,128,768]{2,1,0:T(8,128)(2,1)} %up_i.1, bf16[2,768,128]{2,1,0:T(8,128)(2,1)} %down_i.1, bf16[128,2048]{1,0:T(8,128)(2,1)} %tok_i.1, s32[4,128]{1,0:T(4,128)} %bitcast.12, s32[4,128]{1,0:T(4,128)} %bitcast.13, f32[4,128]{1,0:T(4,128)} %bitcast.14, ...), custom_call_target="tpu_custom_call" | custom-call | tf_op jit(solution)/shard_map/main/pallas_call | solution.py:548
  196.3 0.0 copy-start
  196.3 1.4 copy.14
  197.6 0.0 copy-done
  197.6 0.6 copy.15
Async XLA Ops:
  196.3 1.4 copy-start
